TPU v7x, 512 devices: a whole 4x4x16 slice. The times are simulated.
512 devices in a mesh: rows: 64 (over z, y), cols: 8 (over x, core).
Axes of the slice: x: 4, y: 4, z: 16, core: 2. Of those that a mesh axis runs over, the one named last changes fastest.
Arguments:
- x_start: float32 [96, 32768], P('cols', 'rows'), may hold values from -6 to 6
- p_start: float32 [96, 32768], P('cols', 'rows'), may hold values from -6 to 6
- k_diag: bfloat16 [512, 64, 64], P('rows'), as said below
- k_link: bfloat16 [512, 4, 64, 64], P('rows')
- m_diag: bfloat16 [512, 64, 64], P('rows'), as said below
- m_link: bfloat16 [512, 4, 64, 64], P('rows')
- link_to: int32 [512, 4], P('rows'), may hold values from 0 to 7, as said below
- link_count: int32 [512], P('rows'), may hold values from 1 to 4, as said below
- k_iface: bfloat16 [64, 64, 3, 64, 64], P('rows'), as said below
- m_iface: bfloat16 [64, 64, 3, 64, 64], P('rows'), as said below
- iface_local: int32 [64, 64, 3], P('rows'), may hold values from 0 to 7, as said below
- iface_live: int32 [64, 64, 3], P('rows'), may hold values from 0 to 1, as said below
Outputs:
- x_out: float32 [96, 32768], P('cols', 'rows')
- p_out: float32 [96, 32768], P('cols', 'rows')
- ritz: float32 [96, 96], replicated
Inputs may be any that keep to these rules, and one draw needn't show every extreme that they name: `link_to`: for each row owner and each b < 4, the b-th links of its 8 supernodes form a permutation of its supernodes. `link_count`: the first supernode of every row owner has all 4 links live. `iface_local`: each row owner's 192 slots name each of its supernodes at most (199) // 8 times. iface_live[p, q, c] = iface_live[q, p, c], and it is 0 where p = q. `k_iface`: for p < q the block for (q, p, c) is the transpose of the block for (p, q, c). `m_iface`: for p < q the block for (q, p, c) is the transpose of the block for (p, q, c). `k_diag`: every block is symmetric with diagonal entries of 1 or more. `m_diag`: every block is symmetric with diagonal entries of 1 or more.
All inputs are finite; a program needn't handle non-finite values.
Results may differ from a plain program's by a relative error of at most 0.0003.
Values sent between devices are 32-bit elements; how exact they have to be, the bound alone decides.
No kernel may reach another device: no remote copies, remote signals or barrier semaphores. Data moves between devices by JAX's collectives and lax.ppermute only.
A program may use at most 128 MiB of HBM per device.

v0:
```python
import jax
import jax.numpy as jnp
from jax import lax
from jax.sharding import PartitionSpec as P

STEPS = 2
RR_ITERS = 3


exact_dots = lax.Precision.HIGHEST


def symmetric(matrix):
    return 0.5 * (matrix + matrix.T)


def local_product(vectors, diag_blocks, link_blocks, link_onehot, link_live):
    near = (
        jnp.einsum("sbt,ctj->csbj", link_onehot, vectors, precision=exact_dots)
        * link_live[None, :, :, None]
    )
    result = jnp.einsum(
        "sij,csj->csi", diag_blocks.astype(jnp.float32), vectors, precision=exact_dots
    )
    result = result + jnp.einsum(
        "sbij,csbj->csi", link_blocks.astype(jnp.float32), near, precision=exact_dots
    )
    back = (
        jnp.einsum("sbji,csj->csbi", link_blocks.astype(jnp.float32), vectors, precision=exact_dots)
        * link_live[None, :, :, None]
    )
    return result + jnp.einsum("sbt,csbi->cti", link_onehot, back, precision=exact_dots)


def apply_pair(vectors, tables):
    (
        k_diag,
        k_link,
        m_diag,
        m_link,
        link_onehot,
        link_live,
        k_faces,
        m_faces,
        slot_onehot,
        slot_live,
    ) = tables
    col_count, row_count = vectors.shape
    node_count = link_onehot.shape[0]
    node_size = k_diag.shape[1]
    split_vec = vectors.reshape(col_count, node_count, node_size)
    picked = jnp.einsum("ks,csj->kcj", slot_onehot, split_vec, precision=exact_dots)
    owners = lax.axis_size("rows")

    def face_term(faces):
        term = (
            jnp.einsum("kij,kcj->kci", faces.astype(jnp.float32), picked, precision=exact_dots)
            * slot_live[:, None, None]
        )
        return term.reshape(owners, -1)

    recv_k, recv_m = (
        lax.all_to_all(face_term(k_faces), "rows", split_axis=0, concat_axis=0, tiled=True),
        lax.all_to_all(face_term(m_faces), "rows", split_axis=0, concat_axis=0, tiled=True),
    )

    def finish(diag_blocks, link_blocks, received):
        local = local_product(split_vec, diag_blocks, link_blocks, link_onehot, link_live)
        arrived = jnp.einsum(
            "ks,kci->csi",
            slot_onehot,
            received.reshape(-1, col_count, node_size),
            precision=exact_dots,
        )
        return (local + arrived).reshape(col_count, row_count)

    return (finish(k_diag, k_link, recv_k), finish(m_diag, m_link, recv_m))


def gram_pair(own_s, own_k, own_m):
    blocks, col_part, row_count = own_s.shape
    modes = col_part * lax.axis_size("cols")
    dof_count = row_count * lax.axis_size("rows")
    empty = jnp.zeros((blocks, modes, blocks, col_part), jnp.float32)
    panel_rows = lax.all_gather(own_s, "cols", axis=1, tiled=True)
    offset = jnp.int32(0)
    term_k = jnp.einsum("anr,bcr->anbc", panel_rows, own_k, precision=exact_dots)
    term_m = jnp.einsum("anr,bcr->anbc", panel_rows, own_m, precision=exact_dots)
    part_k = lax.dynamic_update_slice_in_dim(empty, term_k, offset, 1)
    part_m = lax.dynamic_update_slice_in_dim(empty, term_m, offset, 1)
    summed_k, summed_m = lax.psum((part_k, part_m), "rows")
    full_k, full_m = (
        lax.all_gather(summed_k, "cols", axis=3, tiled=True),
        lax.all_gather(summed_m, "cols", axis=3, tiled=True),
    )
    extent = blocks * modes
    return (
        symmetric(full_k.reshape(extent, extent) / dof_count),
        symmetric(full_m.reshape(extent, extent) / dof_count),
        own_s,
    )


def rayleigh(gram_stiff, gram_mass, modes):
    total = gram_stiff.shape[0]
    factor = jnp.linalg.cholesky(gram_stiff)
    coeffs = jnp.eye(total, modes, dtype=jnp.float32)
    for inner_index in range(RR_ITERS):
        solved = jax.scipy.linalg.cho_solve(
            (factor, True), jnp.dot(gram_mass, coeffs, precision=exact_dots)
        )
        inner = symmetric(
            jnp.dot(
                solved.T, jnp.dot(gram_mass, solved, precision=exact_dots), precision=exact_dots
            )
        )
        inner_factor = jnp.linalg.cholesky(inner)
        coeffs = jax.scipy.linalg.solve_triangular(inner_factor, solved.T, lower=True).T
    ritz_new = symmetric(
        jnp.dot(coeffs.T, jnp.dot(gram_stiff, coeffs, precision=exact_dots), precision=exact_dots)
    )
    return (coeffs, ritz_new)


def contract(coef, panel_rows):
    new_x = jnp.einsum("anc,anr->cr", coef, panel_rows, precision=exact_dots)
    new_p = jnp.einsum("anc,anr->cr", coef[1:], panel_rows[1:], precision=exact_dots)
    return (new_x, new_p)


def own_columns(coeffs, blocks, col_part):
    modes = coeffs.shape[1]
    col_start = lax.axis_index("cols") * col_part
    return lax.dynamic_slice_in_dim(coeffs.reshape(blocks, modes, modes), col_start, col_part, 2)


def mass_mixture(mass_x, ritz_now):
    col_part, row_count = mass_x.shape
    col_start = lax.axis_index("cols") * col_part
    coef = lax.dynamic_slice_in_dim(ritz_now, col_start, col_part, 1)
    panel_rows = lax.all_gather(mass_x, "cols", axis=0, tiled=True)
    part = lax.slice_in_dim(coef, 0, panel_rows.shape[0], axis=0)
    return jnp.zeros((col_part, row_count), jnp.float32) + jnp.einsum(
        "nc,nr->cr", part, panel_rows, precision=exact_dots
    )


def body(
    x_start,
    p_start,
    k_diag,
    k_link,
    m_diag,
    m_link,
    link_to,
    link_count,
    k_iface,
    m_iface,
    iface_local,
    iface_live,
):
    col_part, row_count = x_start.shape
    modes = col_part * lax.axis_size("cols")
    node_count, link_slots = link_to.shape
    node_size = k_diag.shape[1]
    node_ids = jnp.arange(node_count, dtype=jnp.int32)
    link_onehot = (link_to[:, :, None] == node_ids[None, None, :]).astype(jnp.float32)
    link_live = (jnp.arange(link_slots, dtype=jnp.int32)[None, :] < link_count[:, None]).astype(
        jnp.float32
    )
    local_slots = iface_local.reshape(-1)
    slot_onehot = (local_slots[:, None] == node_ids[None, :]).astype(jnp.float32)
    slot_live = iface_live.reshape(-1).astype(jnp.float32)
    k_faces = k_iface.reshape(-1, node_size, node_size)
    m_faces = m_iface.reshape(-1, node_size, node_size)
    tables = (
        k_diag,
        k_link,
        m_diag,
        m_link,
        link_onehot,
        link_live,
        k_faces,
        m_faces,
        slot_onehot,
        slot_live,
    )
    precond = 1.0 / jnp.diagonal(k_diag.astype(jnp.float32), axis1=1, axis2=2).reshape(-1)
    both_k, both_m = apply_pair(jnp.concatenate([x_start, p_start], 0), tables)
    stiff_x, stiff_p = (both_k[:col_part], both_k[col_part:])
    mass_x, mass_p = (both_m[:col_part], both_m[col_part:])
    x_block, p_block = (x_start, p_start)
    stiff_gram, mass_gram, unused = gram_pair(x_block[None], stiff_x[None], mass_x[None])
    ritz_now = jax.scipy.linalg.cho_solve((jnp.linalg.cholesky(mass_gram), True), stiff_gram)
    for step_index in range(STEPS):
        resid = stiff_x - mass_mixture(mass_x, ritz_now)
        search = resid * precond[None, :]
        stiff_w, mass_w = apply_pair(search, tables)
        own_s = jnp.stack([x_block, search, p_block], 0)
        own_k = jnp.stack([stiff_x, stiff_w, stiff_p], 0)
        own_m = jnp.stack([mass_x, mass_w, mass_p], 0)
        gram_stiff, gram_mass, whole = gram_pair(own_s, own_k, own_m)
        coeffs, ritz_new = rayleigh(gram_stiff, gram_mass, modes)
        mine = own_columns(coeffs, 3, col_part)
        empty = jnp.zeros((col_part, row_count), jnp.float32)
        panel_rows = lax.all_gather(own_s, "cols", axis=1, tiled=True)
        add_coef = lax.slice_in_dim(mine, 0, panel_rows.shape[1], axis=1)
        new_x, new_p = contract(add_coef, panel_rows)
        x_block = empty + new_x
        p_block = empty + new_p
        if step_index + 1 < STEPS:
            blank = jnp.zeros((col_part, row_count), jnp.float32)
            panels = (
                lax.all_gather(own_k, "cols", axis=1, tiled=True),
                lax.all_gather(own_m, "cols", axis=1, tiled=True),
            )
            coef = lax.slice_in_dim(mine, 0, panels[0].shape[1], axis=1)
            new_kx, new_kp = contract(coef, panels[0])
            new_mx, new_mp = contract(coef, panels[1])
            stiff_x = blank + new_kx
            stiff_p = blank + new_kp
            mass_x = blank + new_mx
            mass_p = blank + new_mp
        ritz_now = ritz_new
    return (x_block, p_block, ritz_now)


def solution(mesh):
    placed = (
        P("cols", "rows"),
        P("cols", "rows"),
        P("rows", None, None),
        P("rows", None, None, None),
        P("rows", None, None),
        P("rows", None, None, None),
        P("rows", None),
        P("rows"),
        P("rows", None, None, None, None),
        P("rows", None, None, None, None),
        P("rows", None, None),
        P("rows", None, None),
    )
    return jax.shard_map(
        body,
        mesh=mesh,
        in_specs=placed,
        out_specs=(P("cols", "rows"), P("cols", "rows"), P()),
        check_vma=False,
    )
```

profile of v0, /device:TPU:1, one launch (start us, length us, event | category | flops | bytes accessed | tf_op | source)
XLA Modules:
  0.0 1823.3 jit_solution(2422586496049059222)
XLA Ops:
  27.0 19.5 %all-to-all-start.1 = ((f32[64,1,4608]{2,1,0:T(1,128)}), f32[64,1,4608]{2,1,0:T(1,128)}, u32[]{:S(2)}, u32[]{:S(2)}) async-start(f32[64,1,4608]{2,1,0:T(1,128)} %all_to_all.49), calls=%async_computation.1 | async-start | bytes 2359296 | tf_op jit(solution)/shard_map/all_to_all | solution.py:64
  57.7 45.7 %all-to-all-done.1 = f32[64,1,4608]{2,1,0:T(1,128)} async-done(((f32[64,1,4608]{2,1,0:T(1,128)}), f32[64,1,4608]{2,1,0:T(1,128)}, u32[]{:S(2)}, u32[]{:S(2)}) %all-to-all-start.1) | async-done | bytes 1179680 | tf_op jit(solution)/shard_map/all_to_all | solution.py:64
  114.1 15.6 all-gather.1
  183.8 222.6 %all-reduce.5 = (f32[1,96,1,12]{1,3,2,0:T(8,128)S(1)}, f32[1,96,1,12]{1,3,2,0:T(8,128)S(1)}) all-reduce(f32[1,96,1,12]{1,3,2,0:T(8,128)S(1)} %convolution_bitcast_fusion.19, f32[1,96,1,12]{1,3,2,0:T(8,128)S(1)} %convolution_bitcast_fusion.20), channel_id=1, replica_groups=mesh['rows'=64,'cols'=8] {'rows'}, use_global_device_ids=true, to_apply=%region_3.5 | all-reduce | flops 2304 | bytes 18432 | tf_op jit(solution)/shard_map/psum | solution.py:91
  406.3 71.9 %all_gather.42 = f32[1,96,1,96]{1,2,0,3:T(1,128)S(1)} all-gather(f32[1,96,1,12]{1,2,0,3:T(1,128)S(1)} %copy.371), channel_id=1, replica_groups=mesh['rows'=64,'cols'=8] {'cols'}, dimensions={3}, use_global_device_ids=true | all-gather | bytes 41472 | tf_op jit(solution)/shard_map/all_gather | solution.py:94
  496.1 12.8 all_gather.43
  510.2 12.8 all-gather.2
  562.8 17.3 all-to-all-done.2
  599.7 16.2 all_gather.45
  642.4 14.5 all_gather.48
  656.9 13.4 all_gather.49
  673.4 234.2 %all-reduce.11.cloned.1.call-done = (f32[3,96,3,12]{1,3,2,0:T(8,128)}, f32[3,96,3,12]{1,3,2,0:T(8,128)}) async-done(((f32[3,96,3,12]{1,3,2,0:T(8,128)}, f32[3,96,3,12]{1,3,2,0:T(8,128)}), (f32[3,96,3,12]{1,3,2,0:T(8,128)}, f32[3,96,3,12]{1,3,2,0:T(8,128)})) %all-reduce.11.cloned.1.call-update) | async-done | bytes 82960 | tf_op jit(solution)/shard_map/psum | solution.py:91
  908.5 25.0 %all_gather.46 = f32[3,96,3,96]{1,2,0,3:T(4,128)} all-gather(f32[3,96,3,12]{1,2,0,3:T(4,128)S(1)} %copy.399), channel_id=1, replica_groups=mesh['rows'=64,'cols'=8] {'cols'}, dimensions={3}, use_global_device_ids=true | all-gather | bytes 373248 | tf_op jit(solution)/shard_map/all_gather | solution.py:93
  973.0 11.7 cholesky.361
  1012.4 29.5 %custom-call.52 = f32[3,128,128]{1,2,0:T(8,128)S(1)} custom-call(f32[3,128,128]{2,1,0:T(8,128)S(1)} %pad_maximum_fusion), custom_call_target="InvertDiagBlocksLowerTriangular" | custom-call | tf_op jit(solution)/shard_map/jit(_cho_solve)/triangular_solve | solution.py:109
  1042.8 14.3 all_gather.47
  1170.4 13.0 all-gather.3
  1228.7 15.0 all-to-all-done.4
  1262.0 15.7 all_gather.51
  1304.6 248.9 %all-reduce.9.cloned.1.call-done = (f32[3,96,3,12]{1,3,2,0:T(8,128)}, f32[3,96,3,12]{1,3,2,0:T(8,128)}) async-done(((f32[3,96,3,12]{1,3,2,0:T(8,128)}, f32[3,96,3,12]{1,3,2,0:T(8,128)}), (f32[3,96,3,12]{1,3,2,0:T(8,128)}, f32[3,96,3,12]{1,3,2,0:T(8,128)})) %all-reduce.9.cloned.1.call-update) | async-done | bytes 82960 | tf_op jit(solution)/shard_map/psum | solution.py:91
  1554.4 25.0 %all_gather.52 = f32[3,96,3,96]{1,2,0,3:T(4,128)} all-gather(f32[3,96,3,12]{1,2,0,3:T(4,128)S(1)} %copy.458), channel_id=1, replica_groups=mesh['rows'=64,'cols'=8] {'cols'}, dimensions={3}, use_global_device_ids=true | all-gather | bytes 373248 | tf_op jit(solution)/shard_map/all_gather | solution.py:93
  1618.9 11.7 cholesky.451
  1658.3 29.5 %custom-call.60 = f32[3,128,128]{1,2,0:T(8,128)S(1)} custom-call(f32[3,128,128]{2,1,0:T(8,128)S(1)} %pad_maximum_fusion.1), custom_call_target="InvertDiagBlocksLowerTriangular" | custom-call | tf_op jit(solution)/shard_map/jit(_cho_solve)/triangular_solve | solution.py:109
  1688.7 14.3 all_gather.53
  (541 shorter events, 665.1 us)
Async XLA Ops:
  7.2 39.4 %copy-start = (bf16[1,64,3,64,64]{4,3,2,1,0:T(8,128)(2,1)S(1)}, bf16[1,64,3,64,64]{4,3,2,1,0:T(8,128)(2,1)}, u32[]{:S(2)}) copy-start(bf16[1,64,3,64,64]{4,3,2,1,0:T(8,128)(2,1)} %param.26) | copy-start | bytes 4718596
  8.2 516.8 %copy-start.48 = (s32[192]{0:T(256)}, s32[192]{0:T(256)S(1)}, u32[]{:S(2)}) copy-start(s32[192]{0:T(256)S(1)} %eq.37) | copy-start | bytes 2308
  14.4 32.2 %copy-start.54 = (f32[192]{0:T(256)}, f32[192]{0:T(256)S(1)}, u32[]{:S(2)}) copy-start(f32[192]{0:T(256)S(1)} %convert_element_type.19) | copy-start | bytes 2308
  27.0 76.3 %all-to-all-start.1 = ((f32[64,1,4608]{2,1,0:T(1,128)}), f32[64,1,4608]{2,1,0:T(1,128)}, u32[]{:S(2)}, u32[]{:S(2)}) async-start(f32[64,1,4608]{2,1,0:T(1,128)} %all_to_all.49), calls=%async_computation.1 | async-start | bytes 2359296 | tf_op jit(solution)/shard_map/all_to_all | solution.py:64
  57.7 56.3 %copy-start.58 = (s32[8]{0:T(128)S(1)}, s32[8]{0:T(128)}, u32[]{:S(2)}) copy-start(s32[8]{0:T(128)} %param.25) | copy-start | bytes 100
  57.7 56.4 %copy-start.31 = (f32[12,512]{1,0:T(8,128)S(1)}, f32[12,512]{1,0:T(8,128)}, u32[]{:S(2)}) copy-start(f32[12,512]{1,0:T(8,128)} %param.18) | copy-start | bytes 73732
  57.7 73.7 %copy-start.11 = (bf16[8,64,64]{2,1,0:T(8,128)(2,1)S(1)}, bf16[8,64,64]{2,1,0:T(8,128)(2,1)}, u32[]{:S(2)}) copy-start(bf16[8,64,64]{2,1,0:T(8,128)(2,1)} %param.20) | copy-start | bytes 196612
  103.3 65.9 %all-to-all-start = ((f32[64,1,4608]{2,1,0:T(1,128)}), f32[64,1,4608]{2,1,0:T(1,128)}, u32[]{:S(2)}, u32[]{:S(2)}) async-start(f32[64,1,4608]{2,1,0:T(1,128)} %all_to_all.48), calls=%async_computation | async-start | bytes 2359296 | tf_op jit(solution)/shard_map/all_to_all | solution.py:63
  114.0 481.8 %copy-start.52 = (f32[8,4]{0,1:T(4,128)}, f32[8,4]{0,1:T(4,128)S(1)}, u32[]{:S(2)}) copy-start(f32[8,4]{0,1:T(4,128)S(1)} %fusion.359) | copy-start | bytes 388
  114.1 479.4 %copy-start.43 = (f32[8,4]{1,0:T(8,128)}, f32[8,4]{1,0:T(8,128)S(1)}, u32[]{:S(2)}) copy-start(f32[8,4]{1,0:T(8,128)S(1)} %copy.351) | copy-start | bytes 388
  180.7 329.6 %copy-start.33 = (f32[1,12,512]{2,1,0:T(8,128)S(1)}, f32[1,12,512]{2,1,0:T(8,128)}, u32[]{:S(2)}) copy-start(f32[1,12,512]{2,1,0:T(8,128)} %reshape.261) | copy-start | bytes 73732
  540.0 40.0 %all-to-all-start.2 = ((f32[64,1,2304]{2,1,0:T(1,128)}), f32[64,1,2304]{2,1,0:T(1,128)}, u32[]{:S(2)}, u32[]{:S(2)}) async-start(f32[64,1,2304]{2,1,0:T(1,128)} %all_to_all.50), calls=%async_computation.2 | async-start | bytes 1179648 | tf_op jit(solution)/shard_map/all_to_all | solution.py:63
  562.8 34.2 %copy-start.12 = (bf16[8,64,64]{2,1,0:T(8,128)(2,1)S(1)}, bf16[8,64,64]{2,1,0:T(8,128)(2,1)}, u32[]{:S(2)}) copy-start(bf16[8,64,64]{2,1,0:T(8,128)(2,1)} %param.20) | copy-start | bytes 196612
  580.1 49.1 %all-to-all-start.3 = ((f32[64,1,2304]{2,1,0:T(1,128)}), f32[64,1,2304]{2,1,0:T(1,128)}, u32[]{:S(2)}, u32[]{:S(2)}) async-start(f32[64,1,2304]{2,1,0:T(1,128)} %all_to_all.51), calls=%async_computation.3 | async-start | bytes 1179648 | tf_op jit(solution)/shard_map/all_to_all | solution.py:64
  587.6 320.0 %all-reduce.11.cloned.1.call-start = ((), (), s32[]{:S(2)}) async-start(), calls=%async_computation.7 | async-start | bytes 294912 | tf_op jit(solution)/shard_map/psum | solution.py:91
  947.7 57.5 %copy-start.61 = (s32[2]{0:T(128)S(1)}, s32[2]{0:T(128)}, u32[]{:S(2)}) copy-start(s32[2]{0:T(128)} %iota_multiply_fusion) | copy-start | bytes 28
  960.3 51.5 %copy-start.17 = (f32[128,96]{1,0:T(8,128)S(1)}, f32[128,96]{1,0:T(8,128)}, u32[]{:S(2)}) copy-start(f32[128,96]{1,0:T(8,128)} %pad_convert_fusion) | copy-start | bytes 147460
  1141.0 12.7 copy-start.16
  1201.1 42.7 %all-to-all-start.4 = ((f32[64,1,2304]{2,1,0:T(1,128)}), f32[64,1,2304]{2,1,0:T(1,128)}, u32[]{:S(2)}, u32[]{:S(2)}) async-start(f32[64,1,2304]{2,1,0:T(1,128)} %all_to_all.52), calls=%async_computation.4 | async-start | bytes 1179648 | tf_op jit(solution)/shard_map/all_to_all | solution.py:63
  1228.7 26.5 %copy-start.53 = (f32[8,4]{0,1:T(4,128)S(1)}, f32[8,4]{0,1:T(4,128)}, u32[]{:S(2)}) copy-start(f32[8,4]{0,1:T(4,128)} %copy-done.52) | copy-start | bytes 388
  1243.7 43.8 %all-to-all-start.5 = ((f32[64,1,2304]{2,1,0:T(1,128)}), f32[64,1,2304]{2,1,0:T(1,128)}, u32[]{:S(2)}, u32[]{:S(2)}) async-start(f32[64,1,2304]{2,1,0:T(1,128)} %all_to_all.53), calls=%async_computation.5 | async-start | bytes 1179648 | tf_op jit(solution)/shard_map/all_to_all | solution.py:64
  1251.3 302.2 %all-reduce.9.cloned.1.call-start = ((), (), s32[]{:S(2)}) async-start(), calls=%async_computation.6 | async-start | bytes 294912 | tf_op jit(solution)/shard_map/psum | solution.py:91
  1593.6 58.8 %copy-start.60 = (s32[2,2]{1,0:T(2,128)S(1)}, s32[2,2]{1,0:T(2,128)}, u32[]{:S(2)}) copy-start(s32[2,2]{1,0:T(2,128)} %copy-done.59) | copy-start | bytes 52
  1606.1 52.1 %copy-start.18 = (f32[128,96]{1,0:T(8,128)S(1)}, f32[128,96]{1,0:T(8,128)}, u32[]{:S(2)}) copy-start(f32[128,96]{1,0:T(8,128)} %pad_convert_fusion) | copy-start | bytes 147460
  (46 other events, 155.7 us)
Sparse Core Ops, SparseCore 0:
  657.0 250.5 all-reduce.10
  1302.6 250.8 all-reduce.8
where the time goes:
time: 1840 us; the launch traced here: 1820 us
  waiting for transfers between devices  573 us (31%)
  blocking collectives  487 us (26%)
  other arithmetic  339 us (18%)
  matrix products  201 us (11%)
  local copies, waits for them, and re-layouts  144 us (8%)
  starting transfers between devices  60.1 us (3%)
  between operations  19.9 us (1%)
    psum x2, waiting for transfers between devices, gram_pair(): summed_k, summed_m = lax.psum((part_k, part_m), 'rows')  483 us
    psum x1, blocking collectives, gram_pair(): summed_k, summed_m = lax.psum((part_k, part_m), 'rows')  223 us
    all_gather x3, blocking collectives, gram_pair(): lax.all_gather(summed_m, 'cols', axis=3, tiled=True)  100 us
    another operation x21, other arithmetic, rayleigh(): factor = jnp.linalg.cholesky(gram_stiff)  98.4 us
    all_gather x3, blocking collectives, gram_pair(): lax.all_gather(summed_k, 'cols', axis=3, tiled=True)  62.8 us
    another operation x11, other arithmetic, rayleigh(): jax.scipy.linalg.cho_solve((factor, True), jnp.dot(gram_mass, coeffs, pre...  62.4 us
    another operation x18, other arithmetic, rayleigh(): inner_factor = jnp.linalg.cholesky(inner)  60.2 us
    another operation x12, other arithmetic, rayleigh(): jax.scipy.linalg.solve_triangular(inner_factor, solved.T, lower=True)  53.7 us
  transfers between devices with their start and end apart: 8, of which 6 were waited for; matrix products, arithmetic and copies ran while one was open for 6% of the time, Pallas kernels for 0%

commit v1 on v0

v1 whole, which is shorter than its diff:
```python
import jax
import jax.numpy as jnp
from jax import lax
from jax.sharding import PartitionSpec as P

STEPS = 2
RR_ITERS = 3


exact_dots = lax.Precision.HIGHEST


def symmetric(matrix):
    return 0.5 * (matrix + matrix.T)


def edot(a, b):
    return jnp.dot(a, b, precision=exact_dots)


def split_three(values):
    high = lax.reduce_precision(values, 8, 7)
    rest = values - high
    middle = lax.reduce_precision(rest, 8, 7)
    low = rest - middle
    return (high, middle, low)


def swap(array, axis):
    return lax.all_to_all(array, axis, split_axis=0, concat_axis=0, tiled=True)


def spread(array, axis):
    count = lax.axis_size(axis)
    return swap(jnp.broadcast_to(array[None], (count,) + array.shape), axis)


def exchange(vectors, slot_ids, node_count):
    col_count, row_count = vectors.shape
    by_node = jnp.transpose(vectors.reshape(col_count, node_count, -1), (1, 0, 2)).reshape(
        node_count, -1
    )
    picked = jnp.zeros((slot_ids.shape[0], by_node.shape[1]), jnp.float32)
    for node in range(node_count):
        picked = jnp.where(slot_ids[:, None] == node, by_node[node][None, :], picked)
    owners = lax.axis_size("rows")
    received = swap(picked.reshape(owners, -1), "rows")
    return received.reshape(slot_ids.shape[0], col_count, -1)


def apply_pair(vectors, received, tables):
    blocks, src_onehot, dst_onehot, node_count = tables
    col_count, row_count = vectors.shape
    by_node = jnp.transpose(vectors.reshape(col_count, node_count, -1), (1, 0, 2))
    near = jnp.einsum("ks,scj->kcj", src_onehot, by_node, precision=exact_dots)
    sources = jnp.concatenate([received, near], 0)
    stacked = jnp.concatenate(split_three(sources), 1).astype(jnp.bfloat16)
    products = jnp.einsum("kcj,kjn->kcn", stacked, blocks, preferred_element_type=jnp.float32)
    products = (
        products[:, :col_count]
        + products[:, col_count : 2 * col_count]
        + products[:, 2 * col_count :]
    )
    sums = jnp.einsum("ks,kcn->csn", dst_onehot, products, precision=exact_dots)
    half = sums.shape[2] // 2
    return (
        sums[:, :, :half].reshape(col_count, row_count),
        sums[:, :, half:].reshape(col_count, row_count),
    )


def reduce_gram(rows, own_k, own_m, dof_count):
    part = jnp.einsum(
        "nr,cr->nc", rows, jnp.concatenate([own_k, own_m], 0), precision=exact_dots
    )
    extent, width = part.shape
    owners = lax.axis_size("rows")
    summed = jnp.sum(swap(part.reshape(owners, -1), "rows"), 0)
    whole = spread(spread(summed, "rows").reshape(-1), "cols")
    col_count = own_k.shape[0]
    whole = whole.reshape(-1, extent, 2, col_count)
    whole = jnp.transpose(whole, (2, 1, 0, 3)).reshape(2, extent, -1) / dof_count
    return whole[0], whole[1]


def rayleigh(gram_stiff, gram_mass, modes):
    total = gram_stiff.shape[0]
    factor = jnp.linalg.cholesky(gram_stiff)
    coeffs = jnp.eye(total, modes, dtype=jnp.float32)
    for inner_index in range(RR_ITERS):
        solved = jax.scipy.linalg.cho_solve((factor, True), edot(gram_mass, coeffs))
        inner = symmetric(edot(solved.T, edot(gram_mass, solved)))
        inner_factor = jnp.linalg.cholesky(inner)
        coeffs = jax.scipy.linalg.solve_triangular(inner_factor, solved.T, lower=True).T
    ritz_new = symmetric(edot(coeffs.T, edot(gram_stiff, coeffs)))
    return (coeffs, ritz_new)


def assemble(xx, xp, pp, column):
    modes = xx.shape[0]
    xw = column[:modes]
    ww = symmetric(column[modes : 2 * modes])
    pw = column[2 * modes :]
    return jnp.concatenate(
        [
            jnp.concatenate([xx, xw, xp], 1),
            jnp.concatenate([xw.T, ww, pw.T], 1),
            jnp.concatenate([xp.T, pw, pp], 1),
        ],
        0,
    )


def body(
    x_start,
    p_start,
    k_diag,
    k_link,
    m_diag,
    m_link,
    link_to,
    link_count,
    k_iface,
    m_iface,
    iface_local,
    iface_live,
):
    col_part, row_count = x_start.shape
    modes = col_part * lax.axis_size("cols")
    dof_count = row_count * lax.axis_size("rows")
    node_count, link_slots = link_to.shape
    node_size = k_diag.shape[1]
    node_ids = jnp.arange(node_count, dtype=jnp.int32)
    slot_ids = iface_local.reshape(-1)
    slot_live = iface_live.reshape(-1) > 0
    link_live = jnp.arange(link_slots, dtype=jnp.int32)[None, :] < link_count[:, None]

    def side_by_side(k_part, m_part, live):
        pair = jnp.concatenate([k_part, m_part], 2)
        return jnp.where(live[:, None, None], pair, jnp.zeros_like(pair))

    def flat(blocks):
        return blocks.reshape(-1, node_size, node_size)

    def flipped(blocks):
        return jnp.swapaxes(flat(blocks), 1, 2)

    live_flat = link_live.reshape(-1)
    blocks = jnp.concatenate(
        [
            side_by_side(flat(k_iface), flat(m_iface), slot_live),
            side_by_side(k_diag, m_diag, jnp.ones((node_count,), bool)),
            side_by_side(flipped(k_link), flipped(m_link), live_flat),
            side_by_side(flat(k_link), flat(m_link), live_flat),
        ],
        0,
    )
    link_from = jnp.repeat(node_ids, link_slots)
    link_flat = link_to.reshape(-1)
    src_ids = jnp.concatenate([node_ids, link_flat, link_from])
    dst_ids = jnp.concatenate([slot_ids, node_ids, link_from, link_flat])
    src_onehot = (src_ids[:, None] == node_ids[None, :]).astype(jnp.float32)
    dst_onehot = (dst_ids[:, None] == node_ids[None, :]).astype(jnp.float32)
    tables = (blocks, src_onehot, dst_onehot, node_count)

    precond = 1.0 / jnp.diagonal(k_diag.astype(jnp.float32), axis1=1, axis2=2).reshape(-1)
    col_start = lax.axis_index("cols") * col_part

    received_x = exchange(x_start, slot_ids, node_count)
    both = spread(jnp.stack([x_start, p_start]), "cols")
    all_x = both[:, 0].reshape(modes, row_count)
    all_p = both[:, 1].reshape(modes, row_count)
    own_kx, own_mx = apply_pair(x_start, received_x, tables)
    stiff_xx, mass_xx = reduce_gram(all_x, own_kx, own_mx, dof_count)
    stiff_xx, mass_xx = symmetric(stiff_xx), symmetric(mass_xx)
    received_p = exchange(p_start, slot_ids, node_count)
    own_kp, own_mp = apply_pair(p_start, received_p, tables)
    moved = spread(jnp.stack([own_kx, own_mx, own_kp, own_mp]), "cols")
    all_kx, all_mx, all_kp, all_mp = [moved[:, i].reshape(modes, row_count) for i in range(4)]
    stiff_p, mass_p = reduce_gram(
        jnp.concatenate([all_x, all_p], 0), own_kp, own_mp, dof_count
    )
    stiff_xp, stiff_pp = stiff_p[:modes], symmetric(stiff_p[modes:])
    mass_xp, mass_pp = mass_p[:modes], symmetric(mass_p[modes:])

    ritz_now = jax.scipy.linalg.cho_solve((jnp.linalg.cholesky(mass_xx), True), stiff_xx)
    for step_index in range(STEPS):
        all_w = (all_kx - edot(ritz_now.T, all_mx)) * precond[None, :]
        own_w = lax.dynamic_slice_in_dim(all_w, col_start, col_part, 0)
        received_w = exchange(own_w, slot_ids, node_count)
        own_kw, own_mw = apply_pair(own_w, received_w, tables)
        space = jnp.concatenate([all_x, all_w, all_p], 0)
        stiff_w, mass_w = reduce_gram(space, own_kw, own_mw, dof_count)
        gram_stiff = assemble(stiff_xx, stiff_xp, stiff_pp, stiff_w)
        gram_mass = assemble(mass_xx, mass_xp, mass_pp, mass_w)
        coeffs, ritz_now = rayleigh(gram_stiff, gram_mass, modes)
        if step_index + 1 == STEPS:
            mine = lax.dynamic_slice_in_dim(coeffs, col_start, col_part, 1)
            p_out = edot(mine[modes:].T, space[modes:])
            x_out = p_out + edot(mine[:modes].T, space[:modes])
            return (x_out, p_out, ritz_now)
        moved = spread(jnp.stack([own_kw, own_mw]), "cols")
        all_kw, all_mw = [moved[:, i].reshape(modes, row_count) for i in range(2)]
        wide = jnp.concatenate(
            [
                space,
                jnp.concatenate([all_kx, all_kw, all_kp], 0),
                jnp.concatenate([all_mx, all_mw, all_mp], 0),
            ],
            1,
        )
        new_p = edot(coeffs[modes:].T, wide[modes:])
        new_x = new_p + edot(coeffs[:modes].T, wide[:modes])
        all_x, all_kx, all_mx = [new_x[:, i * row_count : (i + 1) * row_count] for i in range(3)]
        all_p, all_kp, all_mp = [new_p[:, i * row_count : (i + 1) * row_count] for i in range(3)]
        tail = coeffs.at[:modes].set(0.0)
        pair = jnp.concatenate([coeffs, tail], 1)
        next_stiff = symmetric(edot(pair.T, edot(gram_stiff, pair)))
        next_mass = symmetric(edot(pair.T, edot(gram_mass, pair)))
        stiff_xx, stiff_xp, stiff_pp = (
            next_stiff[:modes, :modes],
            next_stiff[:modes, modes:],
            next_stiff[modes:, modes:],
        )
        mass_xx, mass_xp, mass_pp = (
            next_mass[:modes, :modes],
            next_mass[:modes, modes:],
            next_mass[modes:, modes:],
        )


def solution(mesh):
    placed = (
        P("cols", "rows"),
        P("cols", "rows"),
        P("rows", None, None),
        P("rows", None, None, None),
        P("rows", None, None),
        P("rows", None, None, None),
        P("rows", None),
        P("rows"),
        P("rows", None, None, None, None),
        P("rows", None, None, None, None),
        P("rows", None, None),
        P("rows", None, None),
    )
    return jax.shard_map(
        body,
        mesh=mesh,
        in_specs=placed,
        out_specs=(P("cols", "rows"), P("cols", "rows"), P()),
        check_vma=False,
    )
```

time: 1840 us -> 855 us (0.46)
  blocking collectives: 487 us -> 0 us
  waiting for transfers between devices: 573 us -> 188 us
  matrix products: 201 us -> 79.1 us
  starting transfers between devices: 60.1 us -> 142 us
  local copies, waits for them, and re-layouts: 144 us -> 106 us
    psum x2 -> x0, waiting for transfers between devices: 483 us -> none  [gram_pair(): summed_k, summed_m = lax.psum((part_k, part_m), 'rows')]
    all_gather x13 -> x0, blocking collectives: 264 us -> none  [the longest x3 100 us: gram_pair(): lax.all_gather(summed_m, 'cols', axis=3, tiled=True)]
    psum x1 -> x0, blocking collectives: 223 us -> none  [gram_pair(): summed_k, summed_m = lax.psum((part_k, part_m), 'rows')]
    all_to_all x6 -> x19, waiting for transfers between devices: 89.7 us -> 188 us  [swap(): return lax.all_to_all(array, axis, split_axis=0, concat_axis=0, tiled=True)]
    dot_general x80 -> x48, matrix products: 155 us -> 59.7 us  [the longest x4 27 us: apply_pair(): jnp.einsum('kcj,kjn->kcn', stacked, blocks, preferred_element_type=jnp.fl...]
    all_to_all x6 -> x19, starting transfers between devices: 60 us -> 142 us  [swap(): return lax.all_to_all(array, axis, split_axis=0, concat_axis=0, tiled=True)]
    another operation x62, matrix products: 33.9 us -> 14.9 us  [the longest x60 14.5 us: rayleigh(): solved = jax.scipy.linalg.cho_solve((factor, True), edot(gram_mass, coeffs))]
    another operation x18 -> x23, other arithmetic: 80.7 us -> 83.2 us  [the longest x11 59.8 us: rayleigh(): solved = jax.scipy.linalg.cho_solve((factor, True), edot(gram_mass, coeffs))]
  transfers between devices with their start and end apart: 8 -> 19, of which waited for: 6 -> 17; matrix products, arithmetic and copies ran while one was open for 6% -> 12% of each run, Pallas kernels for 0% -> 0%
where the time goes in v1:
time: 855 us; the launch traced here: 844 us
  other arithmetic  321 us (38%)
  waiting for transfers between devices  188 us (22%)
  starting transfers between devices  142 us (17%)
  local copies, waits for them, and re-layouts  106 us (12%)
  matrix products  79.1 us (9%)
    all_to_all x19, waiting for transfers between devices, swap(): return lax.all_to_all(array, axis, split_axis=0, concat_axis=0, tiled=True)  188 us
    all_to_all x19, starting transfers between devices, swap(): return lax.all_to_all(array, axis, split_axis=0, concat_axis=0, tiled=True)  142 us
    another operation x22, other arithmetic, rayleigh(): factor = jnp.linalg.cholesky(gram_stiff)  96.3 us
    another operation x11, other arithmetic, rayleigh(): solved = jax.scipy.linalg.cho_solve((factor, True), edot(gram_mass, coeffs))  59.8 us
    another operation x18, other arithmetic, rayleigh(): inner_factor = jnp.linalg.cholesky(inner)  57.1 us
    another operation x12, other arithmetic, rayleigh(): jax.scipy.linalg.solve_triangular(inner_factor, solved.T, lower=True)  48.3 us
    dot_general x4, matrix products, apply_pair(): jnp.einsum('kcj,kjn->kcn', stacked, blocks, preferred_element_type=jnp.fl...  27 us
    dot_general x32, matrix products, edot(): return jnp.dot(a, b, precision=exact_dots)  22.9 us
  transfers between devices with their start and end apart: 19, of which 17 were waited for; matrix products, arithmetic and copies ran while one was open for 12% of the time, Pallas kernels for 0%

profile of v1, /device:TPU:1, one launch (start us, length us, event | category | flops | bytes accessed | tf_op | source)
XLA Modules:
  0.0 844.0 jit_solution(11346828223635588908)
XLA Ops:
  2.3 10.2 %all-to-all-start = ((f32[8,2,12,512]{3,1,2,0:T(2,128)}), f32[8,2,12,512]{3,1,2,0:T(2,128)S(1)}, u32[]{:S(2)}, u32[]{:S(2)}) async-start(f32[8,2,12,512]{3,1,2,0:T(2,128)} %broadcast_in_dim.606), calls=%async_computation | async-start | bytes 786432 | tf_op jit(solution)/shard_map/all_to_all | solution.py:30
  22.2 14.3 %all-to-all-start.5 = ((f32[64,1,2304]{2,1,0:T(1,128)}), f32[64,1,2304]{2,1,0:T(1,128)}, u32[]{:S(2)}, u32[]{:S(2)}) async-start(f32[64,1,2304]{2,1,0:T(1,128)} %copy.356), calls=%async_computation.5 | async-start | bytes 1179648 | tf_op jit(solution)/shard_map/all_to_all | solution.py:30
  46.8 23.1 %all-to-all-done.5 = f32[64,1,2304]{2,1,0:T(1,128)} async-done(((f32[64,1,2304]{2,1,0:T(1,128)}), f32[64,1,2304]{2,1,0:T(1,128)}, u32[]{:S(2)}, u32[]{:S(2)}) %all-to-all-start.5) | async-done | bytes 589856 | tf_op jit(solution)/shard_map/all_to_all | solution.py:30
  132.8 12.9 %all-to-all-start.2 = ((f32[64,1,36]{2,1,0:T(1,128)}), f32[64,1,36]{2,1,0:T(1,128)S(1)}, u32[]{:S(2)}, u32[]{:S(2)}) async-start(f32[64,1,36]{2,1,0:T(1,128)} %bitcast.20), calls=%async_computation.2 | async-start | bytes 65536 | tf_op jit(solution)/shard_map/all_to_all | solution.py:30
  145.9 13.1 %all-to-all-done.2 = f32[64,1,36]{2,1,0:T(1,128)S(1)} async-done(((f32[64,1,36]{2,1,0:T(1,128)}), f32[64,1,36]{2,1,0:T(1,128)S(1)}, u32[]{:S(2)}, u32[]{:S(2)}) %all-to-all-start.2) | async-done | bytes 9248 | tf_op jit(solution)/shard_map/all_to_all | solution.py:30
  165.6 12.3 %all-to-all-done.3 = f32[64,1,36]{2,1,0:T(1,128)S(1)} async-done(((f32[64,1,36]{2,1,0:T(1,128)}), f32[64,1,36]{2,1,0:T(1,128)S(1)}, u32[]{:S(2)}, u32[]{:S(2)}) %all-to-all-start.3) | async-done | bytes 9248 | tf_op jit(solution)/shard_map/all_to_all | solution.py:30
  184.8 11.6 %all-to-all-done.11 = f32[64,1,72]{2,1,0:T(1,128)S(1)} async-done(((f32[64,1,72]{2,1,0:T(1,128)}), f32[64,1,72]{2,1,0:T(1,128)S(1)}, u32[]{:S(2)}, u32[]{:S(2)}) %all-to-all-start.11) | async-done | bytes 18464 | tf_op jit(solution)/shard_map/all_to_all | solution.py:30
  197.0 9.9 %all-to-all-start.4 = ((f32[8,1,2304]{2,1,0:T(1,128)}), f32[8,1,2304]{2,1,0:T(1,128)S(1)}, u32[]{:S(2)}, u32[]{:S(2)}) async-start(f32[8,1,2304]{2,1,0:T(1,128)} %broadcast_in_dim.661), calls=%async_computation.4 | async-start | bytes 147456 | tf_op jit(solution)/shard_map/all_to_all | solution.py:30
  260.8 12.8 %all-to-all-start.7 = ((f32[64,1,2304]{2,1,0:T(1,128)}), f32[64,1,2304]{2,1,0:T(1,128)S(1)}, u32[]{:S(2)}, u32[]{:S(2)}) async-start(f32[64,1,2304]{2,1,0:T(1,128)} %copy.368), calls=%async_computation.7 | async-start | bytes 1179648 | tf_op jit(solution)/shard_map/all_to_all | solution.py:30
  280.7 26.6 %all-to-all-done.7 = f32[64,1,2304]{2,1,0:T(1,128)S(1)} async-done(((f32[64,1,2304]{2,1,0:T(1,128)}), f32[64,1,2304]{2,1,0:T(1,128)S(1)}, u32[]{:S(2)}, u32[]{:S(2)}) %all-to-all-start.7) | async-done | bytes 589856 | tf_op jit(solution)/shard_map/all_to_all | solution.py:30
  337.4 12.1 %all-to-all-done.8 = f32[64,1,108]{2,1,0:T(1,128)S(1)} async-done(((f32[64,1,108]{2,1,0:T(1,128)}), f32[64,1,108]{2,1,0:T(1,128)S(1)}, u32[]{:S(2)}, u32[]{:S(2)}) %all-to-all-start.8) | async-done | bytes 27680 | tf_op jit(solution)/shard_map/all_to_all | solution.py:30
  354.8 13.4 %all-to-all-done.9 = f32[64,1,108]{2,1,0:T(1,128)S(1)} async-done(((f32[64,1,108]{2,1,0:T(1,128)}), f32[64,1,108]{2,1,0:T(1,128)S(1)}, u32[]{:S(2)}, u32[]{:S(2)}) %all-to-all-start.9) | async-done | bytes 27680 | tf_op jit(solution)/shard_map/all_to_all | solution.py:30
  405.2 11.7 %cholesky.342 = f32[128,128]{1,0:T(8,128)S(1)} custom-call(f32[128,128]{1,0:T(8,128)S(1)} %cholesky.518), custom_call_target="Cholesky" | custom-call | tf_op jit(solution)/shard_map/jit(cholesky)/cholesky | solution.py:88
  417.0 9.8 %custom-call.46 = f32[1,128,128]{1,2,0:T(8,128)S(1)} custom-call(f32[1,128,128]{2,1,0:T(8,128)S(1)} %get-tuple-element.181), custom_call_target="InvertDiagBlocksLowerTriangular" | custom-call | tf_op jit(solution)/shard_map/jit(cholesky)/cholesky | solution.py:88
  427.4 11.7 %cholesky.361 = f32[128,128]{1,0:T(8,128)S(1)} custom-call(f32[128,128]{1,0:T(8,128)S(1)} %cholesky.522), custom_call_target="Cholesky" | custom-call | tf_op jit(solution)/shard_map/jit(cholesky)/cholesky | solution.py:88
  439.1 10.0 %custom-call.47 = f32[1,128,128]{1,2,0:T(8,128)S(1)} custom-call(f32[1,128,128]{2,1,0:T(8,128)S(1)} %get-tuple-element.178), custom_call_target="InvertDiagBlocksLowerTriangular" | custom-call | tf_op jit(solution)/shard_map/jit(cholesky)/cholesky | solution.py:88
  460.5 29.5 %custom-call.52 = f32[3,128,128]{1,2,0:T(8,128)S(1)} custom-call(f32[3,128,128]{2,1,0:T(8,128)S(1)} %pad_maximum_fusion.11), custom_call_target="InvertDiagBlocksLowerTriangular" | custom-call | tf_op jit(solution)/shard_map/jit(_cho_solve)/triangular_solve | solution.py:91
  581.3 25.1 %all-to-all-done.15 = f32[64,1,2304]{2,1,0:T(1,128)S(1)} async-done(((f32[64,1,2304]{2,1,0:T(1,128)}), f32[64,1,2304]{2,1,0:T(1,128)S(1)}, u32[]{:S(2)}, u32[]{:S(2)}) %all-to-all-start.15) | async-done | bytes 589856 | tf_op jit(solution)/shard_map/all_to_all | solution.py:30
  632.1 13.3 %all-to-all-done.16 = f32[64,1,108]{2,1,0:T(1,128)S(1)} async-done(((f32[64,1,108]{2,1,0:T(1,128)}), f32[64,1,108]{2,1,0:T(1,128)S(1)}, u32[]{:S(2)}, u32[]{:S(2)}) %all-to-all-start.16) | async-done | bytes 27680 | tf_op jit(solution)/shard_map/all_to_all | solution.py:30
  651.5 12.7 %all-to-all-done.17 = f32[64,1,108]{2,1,0:T(1,128)S(1)} async-done(((f32[64,1,108]{2,1,0:T(1,128)}), f32[64,1,108]{2,1,0:T(1,128)S(1)}, u32[]{:S(2)}, u32[]{:S(2)}) %all-to-all-start.17) | async-done | bytes 27680 | tf_op jit(solution)/shard_map/all_to_all | solution.py:30
  689.1 11.7 %cholesky.432 = f32[128,128]{1,0:T(8,128)S(1)} custom-call(f32[128,128]{1,0:T(8,128)S(1)} %cholesky.526), custom_call_target="Cholesky" | custom-call | tf_op jit(solution)/shard_map/jit(cholesky)/cholesky | solution.py:88
  711.2 11.7 %cholesky.451 = f32[128,128]{1,0:T(8,128)S(1)} custom-call(f32[128,128]{1,0:T(8,128)S(1)} %cholesky.530), custom_call_target="Cholesky" | custom-call | tf_op jit(solution)/shard_map/jit(cholesky)/cholesky | solution.py:88
  723.0 10.0 %custom-call.55 = f32[1,128,128]{1,2,0:T(8,128)S(1)} custom-call(f32[1,128,128]{2,1,0:T(8,128)S(1)} %get-tuple-element.173), custom_call_target="InvertDiagBlocksLowerTriangular" | custom-call | tf_op jit(solution)/shard_map/jit(cholesky)/cholesky | solution.py:88
  744.3 29.5 %custom-call.60 = f32[3,128,128]{1,2,0:T(8,128)S(1)} custom-call(f32[3,128,128]{2,1,0:T(8,128)S(1)} %pad_maximum_fusion.12), custom_call_target="InvertDiagBlocksLowerTriangular" | custom-call | tf_op jit(solution)/shard_map/jit(_cho_solve)/triangular_solve | solution.py:91
  (767 shorter events, 484.5 us)
Async XLA Ops:
  2.3 19.9 %all-to-all-start = ((f32[8,2,12,512]{3,1,2,0:T(2,128)}), f32[8,2,12,512]{3,1,2,0:T(2,128)S(1)}, u32[]{:S(2)}, u32[]{:S(2)}) async-start(f32[8,2,12,512]{3,1,2,0:T(2,128)} %broadcast_in_dim.606), calls=%async_computation | async-start | bytes 786432 | tf_op jit(solution)/shard_map/all_to_all | solution.py:30
  16.0 242.8 %copy-start.2 = (pred[64,1,2304]{2,0,1:T(8,128)(4,1)}, pred[64,1,2304]{2,0,1:T(8,128)(4,1)S(1)}, u32[]{:S(2)}) copy-start(pred[64,1,2304]{2,0,1:T(8,128)(4,1)S(1)} %broadcast_in_dim.620) | copy-start | bytes 442372
  16.7 242.1 %copy-start.4 = (pred[64,1,2304]{2,0,1:T(8,128)(4,1)}, pred[64,1,2304]{2,0,1:T(8,128)(4,1)S(1)}, u32[]{:S(2)}) copy-start(pred[64,1,2304]{2,0,1:T(8,128)(4,1)S(1)} %broadcast_in_dim.626) | copy-start | bytes 442372
  17.3 241.5 %copy-start.6 = (pred[64,1,2304]{2,0,1:T(8,128)(4,1)}, pred[64,1,2304]{2,0,1:T(8,128)(4,1)S(1)}, u32[]{:S(2)}) copy-start(pred[64,1,2304]{2,0,1:T(8,128)(4,1)S(1)} %broadcast_in_dim.632) | copy-start | bytes 442372
  18.0 240.8 %copy-start.8 = (pred[64,1,2304]{2,0,1:T(8,128)(4,1)}, pred[64,1,2304]{2,0,1:T(8,128)(4,1)S(1)}, u32[]{:S(2)}) copy-start(pred[64,1,2304]{2,0,1:T(8,128)(4,1)S(1)} %broadcast_in_dim.638) | copy-start | bytes 442372
  18.7 240.2 %copy-start.10 = (pred[64,1,2304]{2,0,1:T(8,128)(4,1)}, pred[64,1,2304]{2,0,1:T(8,128)(4,1)S(1)}, u32[]{:S(2)}) copy-start(pred[64,1,2304]{2,0,1:T(8,128)(4,1)S(1)} %broadcast_in_dim.644) | copy-start | bytes 442372
  22.2 47.8 %all-to-all-start.5 = ((f32[64,1,2304]{2,1,0:T(1,128)}), f32[64,1,2304]{2,1,0:T(1,128)}, u32[]{:S(2)}, u32[]{:S(2)}) async-start(f32[64,1,2304]{2,1,0:T(1,128)} %copy.356), calls=%async_computation.5 | async-start | bytes 1179648 | tf_op jit(solution)/shard_map/all_to_all | solution.py:30
  70.0 39.1 %all-to-all-start.1 = ((f32[64,1,2304]{2,1,0:T(1,128)}), f32[64,1,2304]{2,1,0:T(1,128)}, u32[]{:S(2)}, u32[]{:S(2)}) async-start(f32[64,1,2304]{2,1,0:T(1,128)} %copy.341), calls=%async_computation.1 | async-start | bytes 1179648 | tf_op jit(solution)/shard_map/all_to_all | solution.py:30
  132.8 26.2 %all-to-all-start.2 = ((f32[64,1,36]{2,1,0:T(1,128)}), f32[64,1,36]{2,1,0:T(1,128)S(1)}, u32[]{:S(2)}, u32[]{:S(2)}) async-start(f32[64,1,36]{2,1,0:T(1,128)} %bitcast.20), calls=%async_computation.2 | async-start | bytes 65536 | tf_op jit(solution)/shard_map/all_to_all | solution.py:30
  159.8 18.1 %all-to-all-start.3 = ((f32[64,1,36]{2,1,0:T(1,128)}), f32[64,1,36]{2,1,0:T(1,128)S(1)}, u32[]{:S(2)}, u32[]{:S(2)}) async-start(f32[64,1,36]{2,1,0:T(1,128)} %broadcast_in_dim.659), calls=%async_computation.3 | async-start | bytes 65536 | tf_op jit(solution)/shard_map/all_to_all | solution.py:30
  177.9 18.5 %all-to-all-start.11 = ((f32[64,1,72]{2,1,0:T(1,128)}), f32[64,1,72]{2,1,0:T(1,128)S(1)}, u32[]{:S(2)}, u32[]{:S(2)}) async-start(f32[64,1,72]{2,1,0:T(1,128)} %bitcast.37), calls=%async_computation.11 | async-start | bytes 65536 | tf_op jit(solution)/shard_map/all_to_all | solution.py:30
  197.0 14.8 %all-to-all-start.4 = ((f32[8,1,2304]{2,1,0:T(1,128)}), f32[8,1,2304]{2,1,0:T(1,128)S(1)}, u32[]{:S(2)}, u32[]{:S(2)}) async-start(f32[8,1,2304]{2,1,0:T(1,128)} %broadcast_in_dim.661), calls=%async_computation.4 | async-start | bytes 147456 | tf_op jit(solution)/shard_map/all_to_all | solution.py:30
  212.5 18.1 %all-to-all-start.12 = ((f32[64,1,72]{2,1,0:T(1,128)}), f32[64,1,72]{2,1,0:T(1,128)S(1)}, u32[]{:S(2)}, u32[]{:S(2)}) async-start(f32[64,1,72]{2,1,0:T(1,128)} %broadcast_in_dim.730), calls=%async_computation.12 | async-start | bytes 65536 | tf_op jit(solution)/shard_map/all_to_all | solution.py:30
  231.6 17.5 %all-to-all-start.6 = ((f32[8,4,12,512]{3,1,2,0:T(4,128)}), f32[8,4,12,512]{3,1,2,0:T(4,128)S(1)}, u32[]{:S(2)}, u32[]{:S(2)}) async-start(f32[8,4,12,512]{3,1,2,0:T(4,128)} %broadcast_in_dim.694), calls=%async_computation.6 | async-start | bytes 1572864 | tf_op jit(solution)/shard_map/all_to_all | solution.py:30
  249.9 10.9 %all-to-all-start.13 = ((f32[8,1,4608]{2,1,0:T(1,128)}), f32[8,1,4608]{2,1,0:T(1,128)S(1)}, u32[]{:S(2)}, u32[]{:S(2)}) async-start(f32[8,1,4608]{2,1,0:T(1,128)} %broadcast_in_dim.732), calls=%async_computation.13 | async-start | bytes 294912 | tf_op jit(solution)/shard_map/all_to_all | solution.py:30
  260.8 46.5 %all-to-all-start.7 = ((f32[64,1,2304]{2,1,0:T(1,128)}), f32[64,1,2304]{2,1,0:T(1,128)S(1)}, u32[]{:S(2)}, u32[]{:S(2)}) async-start(f32[64,1,2304]{2,1,0:T(1,128)} %copy.368), calls=%async_computation.7 | async-start | bytes 1179648 | tf_op jit(solution)/shard_map/all_to_all | solution.py:30
  328.3 21.2 %all-to-all-start.8 = ((f32[64,1,108]{2,1,0:T(1,128)}), f32[64,1,108]{2,1,0:T(1,128)S(1)}, u32[]{:S(2)}, u32[]{:S(2)}) async-start(f32[64,1,108]{2,1,0:T(1,128)} %bitcast.33), calls=%async_computation.8 | async-start | bytes 65536 | tf_op jit(solution)/shard_map/all_to_all | solution.py:30
  350.1 18.1 %all-to-all-start.9 = ((f32[64,1,108]{2,1,0:T(1,128)}), f32[64,1,108]{2,1,0:T(1,128)S(1)}, u32[]{:S(2)}, u32[]{:S(2)}) async-start(f32[64,1,108]{2,1,0:T(1,128)} %broadcast_in_dim.727), calls=%async_computation.9 | async-start | bytes 65536 | tf_op jit(solution)/shard_map/all_to_all | solution.py:30
  369.1 16.4 %all-to-all-start.14 = ((f32[8,2,12,512]{3,1,2,0:T(2,128)}), f32[8,2,12,512]{3,1,2,0:T(2,128)S(1)}, u32[]{:S(2)}, u32[]{:S(2)}) async-start(f32[8,2,12,512]{3,1,2,0:T(2,128)} %broadcast_in_dim.733), calls=%async_computation.14 | async-start | bytes 786432 | tf_op jit(solution)/shard_map/all_to_all | solution.py:30
  386.2 10.3 %all-to-all-start.10 = ((f32[8,1,6912]{2,1,0:T(1,128)}), f32[8,1,6912]{2,1,0:T(1,128)S(1)}, u32[]{:S(2)}, u32[]{:S(2)}) async-start(f32[8,1,6912]{2,1,0:T(1,128)} %broadcast_in_dim.729), calls=%async_computation.10 | async-start | bytes 442368 | tf_op jit(solution)/shard_map/all_to_all | solution.py:30
  569.5 37.0 %all-to-all-start.15 = ((f32[64,1,2304]{2,1,0:T(1,128)}), f32[64,1,2304]{2,1,0:T(1,128)S(1)}, u32[]{:S(2)}, u32[]{:S(2)}) async-start(f32[64,1,2304]{2,1,0:T(1,128)} %copy.417), calls=%async_computation.15 | async-start | bytes 1179648 | tf_op jit(solution)/shard_map/all_to_all | solution.py:30
  623.4 22.0 %all-to-all-start.16 = ((f32[64,1,108]{2,1,0:T(1,128)}), f32[64,1,108]{2,1,0:T(1,128)S(1)}, u32[]{:S(2)}, u32[]{:S(2)}) async-start(f32[64,1,108]{2,1,0:T(1,128)} %bitcast.96), calls=%async_computation.16 | async-start | bytes 65536 | tf_op jit(solution)/shard_map/all_to_all | solution.py:30
  646.1 18.1 %all-to-all-start.17 = ((f32[64,1,108]{2,1,0:T(1,128)}), f32[64,1,108]{2,1,0:T(1,128)S(1)}, u32[]{:S(2)}, u32[]{:S(2)}) async-start(f32[64,1,108]{2,1,0:T(1,128)} %broadcast_in_dim.766), calls=%async_computation.17 | async-start | bytes 65536 | tf_op jit(solution)/shard_map/all_to_all | solution.py:30
  665.9 13.7 %all-to-all-start.18 = ((f32[8,1,6912]{2,1,0:T(1,128)}), f32[8,1,6912]{2,1,0:T(1,128)S(1)}, u32[]{:S(2)}, u32[]{:S(2)}) async-start(f32[8,1,6912]{2,1,0:T(1,128)} %broadcast_in_dim.768), calls=%async_computation.18 | async-start | bytes 442368 | tf_op jit(solution)/shard_map/all_to_all | solution.py:30
  (80 other events, 2022.5 us)

commit v2 on v1

--- a/solution.py
+++ b/solution.py
@@ -1,6 +1,8 @@
 import jax
 import jax.numpy as jnp
 from jax import lax
+from jax.experimental import pallas as pl
+from jax.experimental.pallas import tpu as pltpu
 from jax.sharding import PartitionSpec as P
 
 STEPS = 2
@@ -8,10 +10,6 @@
 
 
 exact_dots = lax.Precision.HIGHEST
-
-
-def symmetric(matrix):
-    return 0.5 * (matrix + matrix.T)
 
 
 def edot(a, b):
@@ -70,44 +68,175 @@
 
 
 def reduce_gram(rows, own_k, own_m, dof_count):
-    part = jnp.einsum(
-        "nr,cr->nc", rows, jnp.concatenate([own_k, own_m], 0), precision=exact_dots
-    )
-    extent, width = part.shape
+    own = jnp.concatenate([own_k, own_m], 0)
+    part = jnp.einsum("cr,nr->cn", own, rows, precision=exact_dots) / dof_count
     owners = lax.axis_size("rows")
     summed = jnp.sum(swap(part.reshape(owners, -1), "rows"), 0)
     whole = spread(spread(summed, "rows").reshape(-1), "cols")
-    col_count = own_k.shape[0]
-    whole = whole.reshape(-1, extent, 2, col_count)
-    whole = jnp.transpose(whole, (2, 1, 0, 3)).reshape(2, extent, -1) / dof_count
-    return whole[0], whole[1]
-
-
-def rayleigh(gram_stiff, gram_mass, modes):
-    total = gram_stiff.shape[0]
-    factor = jnp.linalg.cholesky(gram_stiff)
-    coeffs = jnp.eye(total, modes, dtype=jnp.float32)
+    whole = whole.reshape(-1, 2, own_k.shape[0], rows.shape[0])
+    return [whole[:, i].reshape(-1, rows.shape[0]) for i in range(2)]
+
+
+def nn(a, b):
+    return lax.dot_general(
+        a, b, (((1,), (0,)), ((), ())), precision=exact_dots, preferred_element_type=jnp.float32
+    )
+
+
+def nt(a, b):
+    return lax.dot_general(
+        a, b, (((1,), (1,)), ((), ())), precision=exact_dots, preferred_element_type=jnp.float32
+    )
+
+
+LANES = 128
+PANEL = 8
+
+def lower_inverse(matrix, out_ref):
+    size = matrix.shape[0]
+    tiles = size // PANEL
+    wide = jnp.concatenate([matrix, jnp.zeros((size, LANES - size), jnp.float32)], 1)
+    row = lax.broadcasted_iota(jnp.int32, (size, LANES), 0)
+    lane = lax.broadcasted_iota(jnp.int32, (size, LANES), 1)
+    ident = jnp.where(row == lane, 1.0, 0.0).astype(jnp.float32)
+    left = [wide[PANEL * t : PANEL * t + PANEL] for t in range(tiles)]
+    right = [ident[PANEL * t : PANEL * t + PANEL] for t in range(tiles)]
+    full = (PANEL, LANES)
+
+    def lane_splat(tile, k):
+        return jnp.broadcast_to(tile[:, k : k + 1], full)
+
+    def row_splat(tile, i):
+        return jnp.broadcast_to(tile[i : i + 1, :], full)
+
+    for p in range(tiles):
+        base = PANEL * p
+        cols = [lane_splat(left[p], base + k) for k in range(PANEL)]
+        s = {(i, k): row_splat(cols[k], i) for k in range(PANEL) for i in range(k, PANEL)}
+        low = {}
+        inv = {}
+        for k in range(PANEL):
+            d = s[k, k]
+            r = lax.rsqrt(d)
+            r = r * (1.5 - 0.5 * d * r * r)
+            inv[k, k] = r
+            for i in range(k + 1, PANEL):
+                low[i, k] = s[i, k] * r
+            for m in range(k + 1, PANEL):
+                for i in range(m, PANEL):
+                    s[i, m] = s[i, m] - low[i, k] * low[m, k]
+        for i in range(1, PANEL):
+            for j in range(i):
+                acc = low[i, j] * inv[j, j]
+                for k in range(j + 1, i):
+                    acc = acc + low[i, k] * inv[k, j]
+                inv[i, j] = -inv[i, i] * acc
+        rows_l = [row_splat(left[p], i) for i in range(PANEL)]
+        rows_r = [row_splat(right[p], i) for i in range(PANEL)]
+        new_l, new_r = [], []
+        for i in range(PANEL):
+            al = inv[i, 0] * rows_l[0]
+            ar = inv[i, 0] * rows_r[0]
+            for k in range(1, i + 1):
+                al = al + inv[i, k] * rows_l[k]
+                ar = ar + inv[i, k] * rows_r[k]
+            new_l.append(al)
+            new_r.append(ar)
+            out_ref[base + i : base + i + 1, :] = ar[0:1, :size]
+        for t in range(p + 1, tiles):
+            ct = [lane_splat(left[t], base + k) for k in range(PANEL)]
+            for k in range(PANEL):
+                f = inv[k, 0] * ct[0]
+                for j in range(1, k + 1):
+                    f = f + inv[k, j] * ct[j]
+                left[t] = left[t] - f * new_l[k]
+                right[t] = right[t] - f * new_r[k]
+
+
+def first_ritz_kernel(stiff_ref, mass_ref, ritz_ref, tmp_ref):
+    lower_inverse(mass_ref[...], tmp_ref)
+    inv = tmp_ref[...]
+    ritz_ref[...] = nn(nt(stiff_ref[...], inv), inv)
+
+
+def factor_old(stiff, mass, j_ref, jm_ref, b_ref, tmp_ref):
+    n = tmp_ref.shape[0]
+    lower_inverse(stiff[:n, :n], tmp_ref)
+    first = tmp_ref[...]
+    q = nt(stiff[n:, :n], first)
+    lower_inverse(stiff[n:, n:] - nt(q, q), tmp_ref)
+    second = tmp_ref[...]
+    j_ref[:n, :n] = first
+    j_ref[:n, n:] = jnp.zeros((n, n), jnp.float32)
+    j_ref[n:, :n] = -nn(second, nn(q, first))
+    j_ref[n:, n:] = second
+    j = j_ref[...]
+    jm = nt(mass, j)
+    jm_ref[...] = jm
+    b_ref[...] = nn(j, jm)
+
+
+def old_kernel(stiff_ref, mass_ref, j_ref, jm_ref, b_ref, tmp_ref):
+    factor_old(stiff_ref[...], mass_ref[...], j_ref, jm_ref, b_ref, tmp_ref)
+
+
+def carry_kernel(
+    y_ref, gxp_ref, mxp_ref, gw_ref, mw_ref, next_ref, j_ref, jm_ref, b_ref, tmp_ref
+):
+    n = tmp_ref.shape[0]
+    ya = y_ref[:, : 2 * n]
+    yb = y_ref[:, 2 * n :]
+    lane = lax.broadcasted_iota(jnp.int32, ya.shape, 1)
+    pa = jnp.concatenate([ya, jnp.where(lane < n, 0.0, ya)], 0)
+    pb = jnp.concatenate([yb, yb], 0)
+
+    def turned(old_ref, col_ref):
+        col = col_ref[:, : 2 * n]
+        ha = nn(pa, old_ref[...]) + nn(pb, col)
+        hb = nt(pa, col) + nn(pb, col_ref[:, 2 * n :])
+        return nt(ha, pa) + nt(hb, pb)
+
+    mass = turned(mxp_ref, mw_ref)
+    next_ref[...] = mass
+    factor_old(turned(gxp_ref, gw_ref), mass, j_ref, jm_ref, b_ref, tmp_ref)
+
+
+def ritz_kernel(
+    gw_ref, mw_ref, mxp_ref, j_ref, jm_ref, b_ref, y_ref, ritz_ref, tmp_ref
+):
+    n = tmp_ref.shape[0]
+    j = j_ref[...]
+    bxx = b_ref[...]
+    qt = nt(gw_ref[:, : 2 * n], j)
+    lower_inverse(gw_ref[:, 2 * n :] - nt(qt, qt), tmp_ref)
+    lw = tmp_ref[...]
+    t = nn(qt, j)
+    mwx = mw_ref[:, : 2 * n]
+    d = mwx - nn(t, mxp_ref[...])
+    e = mw_ref[:, 2 * n :] - nt(t, mwx) - nt(d, t)
+    bwx = nn(lw, nt(d, j))
+    bww = nt(nn(lw, e), lw)
+    va = jm_ref[:n, :]
+    vb = jnp.transpose(nn(lw, d[:, :n]))
+    ua = ub = None
     for inner_index in range(RR_ITERS):
-        solved = jax.scipy.linalg.cho_solve((factor, True), edot(gram_mass, coeffs))
-        inner = symmetric(edot(solved.T, edot(gram_mass, solved)))
-        inner_factor = jnp.linalg.cholesky(inner)
-        coeffs = jax.scipy.linalg.solve_triangular(inner_factor, solved.T, lower=True).T
-    ritz_new = symmetric(edot(coeffs.T, edot(gram_stiff, coeffs)))
-    return (coeffs, ritz_new)
-
-
-def assemble(xx, xp, pp, column):
-    modes = xx.shape[0]
-    xw = column[:modes]
-    ww = symmetric(column[modes : 2 * modes])
-    pw = column[2 * modes :]
-    return jnp.concatenate(
-        [
-            jnp.concatenate([xx, xw, xp], 1),
-            jnp.concatenate([xw.T, ww, pw.T], 1),
-            jnp.concatenate([xp.T, pw, pp], 1),
-        ],
-        0,
+        wa = nn(va, bxx) + nn(vb, bwx)
+        wb = nt(va, bwx) + nn(vb, bww)
+        lower_inverse(nt(wa, va) + nt(wb, vb), tmp_ref)
+        lc = tmp_ref[...]
+        ua, ub = nn(lc, va), nn(lc, vb)
+        va, vb = nn(lc, wa), nn(lc, wb)
+    ritz_ref[...] = nt(ua, ua) + nt(ub, ub)
+    yw = nn(ub, lw)
+    y_ref[:, : 2 * n] = nn(ua, j) - nn(yw, t)
+    y_ref[:, 2 * n :] = yw
+
+
+def dense(kernel, shapes, size):
+    return pl.pallas_call(
+        kernel,
+        out_shape=tuple(jax.ShapeDtypeStruct(s, jnp.float32) for s in shapes),
+        scratch_shapes=[pltpu.VMEM((size, size), jnp.float32)],
     )
 
 
@@ -166,66 +295,63 @@
     precond = 1.0 / jnp.diagonal(k_diag.astype(jnp.float32), axis1=1, axis2=2).reshape(-1)
     col_start = lax.axis_index("cols") * col_part
 
+    both = spread(jnp.stack([x_start, p_start]), "cols")
     received_x = exchange(x_start, slot_ids, node_count)
-    both = spread(jnp.stack([x_start, p_start]), "cols")
+    received_p = exchange(p_start, slot_ids, node_count)
     all_x = both[:, 0].reshape(modes, row_count)
     all_p = both[:, 1].reshape(modes, row_count)
     own_kx, own_mx = apply_pair(x_start, received_x, tables)
     stiff_xx, mass_xx = reduce_gram(all_x, own_kx, own_mx, dof_count)
-    stiff_xx, mass_xx = symmetric(stiff_xx), symmetric(mass_xx)
-    received_p = exchange(p_start, slot_ids, node_count)
+    moved = spread(jnp.stack([own_kx, own_mx]), "cols")
+    all_kx, all_mx = [moved[:, i].reshape(modes, row_count) for i in range(2)]
     own_kp, own_mp = apply_pair(p_start, received_p, tables)
-    moved = spread(jnp.stack([own_kx, own_mx, own_kp, own_mp]), "cols")
-    all_kx, all_mx, all_kp, all_mp = [moved[:, i].reshape(modes, row_count) for i in range(4)]
     stiff_p, mass_p = reduce_gram(
         jnp.concatenate([all_x, all_p], 0), own_kp, own_mp, dof_count
     )
-    stiff_xp, stiff_pp = stiff_p[:modes], symmetric(stiff_p[modes:])
-    mass_xp, mass_pp = mass_p[:modes], symmetric(mass_p[modes:])
-
-    ritz_now = jax.scipy.linalg.cho_solve((jnp.linalg.cholesky(mass_xx), True), stiff_xx)
+
+    def old_block(xx, column):
+        return jnp.concatenate(
+            [jnp.concatenate([xx, column[:, :modes].T], 1), column], 0
+        )
+
+    square = (modes, modes)
+    pair = (2 * modes, 2 * modes)
+    old_stiff, old_mass = old_block(stiff_xx, stiff_p), old_block(mass_xx, mass_p)
+    factors = dense(old_kernel, (pair,) * 3, modes)(old_stiff, old_mass)
+    (ritz_turned,) = dense(first_ritz_kernel, (square,), modes)(stiff_xx, mass_xx)
     for step_index in range(STEPS):
-        all_w = (all_kx - edot(ritz_now.T, all_mx)) * precond[None, :]
+        all_w = (all_kx - edot(ritz_turned, all_mx)) * precond[None, :]
         own_w = lax.dynamic_slice_in_dim(all_w, col_start, col_part, 0)
         received_w = exchange(own_w, slot_ids, node_count)
         own_kw, own_mw = apply_pair(own_w, received_w, tables)
-        space = jnp.concatenate([all_x, all_w, all_p], 0)
+        space = jnp.concatenate([all_x, all_p, all_w], 0)
         stiff_w, mass_w = reduce_gram(space, own_kw, own_mw, dof_count)
-        gram_stiff = assemble(stiff_xx, stiff_xp, stiff_pp, stiff_w)
-        gram_mass = assemble(mass_xx, mass_xp, mass_pp, mass_w)
-        coeffs, ritz_now = rayleigh(gram_stiff, gram_mass, modes)
+        coeffs, ritz_turned = dense(ritz_kernel, ((modes, 3 * modes), square), modes)(
+            stiff_w, mass_w, old_mass, *factors
+        )
         if step_index + 1 == STEPS:
-            mine = lax.dynamic_slice_in_dim(coeffs, col_start, col_part, 1)
-            p_out = edot(mine[modes:].T, space[modes:])
-            x_out = p_out + edot(mine[:modes].T, space[:modes])
-            return (x_out, p_out, ritz_now)
-        moved = spread(jnp.stack([own_kw, own_mw]), "cols")
-        all_kw, all_mw = [moved[:, i].reshape(modes, row_count) for i in range(2)]
-        wide = jnp.concatenate(
+            mine = lax.dynamic_slice_in_dim(coeffs, col_start, col_part, 0)
+            p_out = edot(mine[:, modes:], space[modes:])
+            x_out = p_out + edot(mine[:, :modes], space[:modes])
+            return (x_out, p_out, ritz_turned)
+        moved = spread(jnp.stack([own_kp, own_mp, own_kw, own_mw]), "cols")
+        all_kp, all_mp, all_kw, all_mw = [
+            moved[:, i].reshape(modes, row_count) for i in range(4)
+        ]
+        wide_x = jnp.concatenate([all_x, all_kx, all_mx], 1)
+        wide_rest = jnp.concatenate(
             [
-                space,
-                jnp.concatenate([all_kx, all_kw, all_kp], 0),
-                jnp.concatenate([all_mx, all_mw, all_mp], 0),
+                jnp.concatenate([all_p, all_kp, all_mp], 1),
+                jnp.concatenate([all_w, all_kw, all_mw], 1),
             ],
-            1,
+            0,
         )
-        new_p = edot(coeffs[modes:].T, wide[modes:])
-        new_x = new_p + edot(coeffs[:modes].T, wide[:modes])
+        new_p = edot(coeffs[:, modes:], wide_rest)
+        new_x = new_p + edot(coeffs[:, :modes], wide_x)
         all_x, all_kx, all_mx = [new_x[:, i * row_count : (i + 1) * row_count] for i in range(3)]
-        all_p, all_kp, all_mp = [new_p[:, i * row_count : (i + 1) * row_count] for i in range(3)]
-        tail = coeffs.at[:modes].set(0.0)
-        pair = jnp.concatenate([coeffs, tail], 1)
-        next_stiff = symmetric(edot(pair.T, edot(gram_stiff, pair)))
-        next_mass = symmetric(edot(pair.T, edot(gram_mass, pair)))
-        stiff_xx, stiff_xp, stiff_pp = (
-            next_stiff[:modes, :modes],
-            next_stiff[:modes, modes:],
-            next_stiff[modes:, modes:],
-        )
-        mass_xx, mass_xp, mass_pp = (
-            next_mass[:modes, :modes],
-            next_mass[:modes, modes:],
-            next_mass[modes:, modes:],
+        all_p = new_p[:, :row_count]
+        old_mass, *factors = dense(carry_kernel, (pair,) * 4, modes)(
+            coeffs, old_stiff, old_mass, stiff_w, mass_w
         )
 
 

time: 855 us -> 565 us (0.66)
  other arithmetic: 321 us -> 34.3 us
  Pallas kernels: 0 us -> 81.2 us
  local copies, waits for them, and re-layouts: 106 us -> 67.3 us
  blocking collectives: 0 us -> 37.3 us
  matrix products: 79.1 us -> 44.2 us
  waiting for transfers between devices: 188 us -> 164 us
  starting transfers between devices: 142 us -> 127 us
    another operation x74 -> x6, other arithmetic: 284 us -> 5.08 us  [the longest x22 96.3 us: rayleigh(): factor = jnp.linalg.cholesky(gram_stiff)]
    pallas_call x0 -> x5, Pallas kernels: none -> 81.2 us  [the longest x2 48.2 us: body(): dense(ritz_kernel, ((modes, 3 * modes), square), modes)]
    all_to_all x0 -> x2, blocking collectives: none -> 37.3 us  [swap(): return lax.all_to_all(array, axis, split_axis=0, concat_axis=0, tiled=True)]
    all_to_all x19 -> x17, waiting for transfers between devices: 188 us -> 164 us  [swap(): return lax.all_to_all(array, axis, split_axis=0, concat_axis=0, tiled=True)]
    another operation x76 -> x0, matrix products: 19.4 us -> none  [the longest x60 14.5 us: rayleigh(): solved = jax.scipy.linalg.cho_solve((factor, True), edot(gram_mass, coeffs))]
    div x8 -> x0, local copies, waits for them, and re-layouts: 16.6 us -> none  [the longest x7 16.5 us: reduce_gram(): jnp.transpose(whole, (2, 1, 0, 3)).reshape(2, extent, -1) / dof_count]
    dot_general x32 -> x6, matrix products: 22.9 us -> 6.63 us  [edot(): return jnp.dot(a, b, precision=exact_dots)]
    all_to_all x19 -> x17, starting transfers between devices: 142 us -> 127 us  [swap(): return lax.all_to_all(array, axis, split_axis=0, concat_axis=0, tiled=True)]
  transfers between devices with their start and end apart: 19 -> 17, of which waited for: 17 -> 13; matrix products, arithmetic and copies ran while one was open for 12% -> 15% of each run, Pallas kernels for 0% -> 10%
where the time goes in v2:
time: 565 us; the launch traced here: 557 us
  waiting for transfers between devices  164 us (29%)
  starting transfers between devices  127 us (22%)
  Pallas kernels  81.2 us (14%)
  local copies, waits for them, and re-layouts  67.3 us (12%)
  matrix products  44.2 us (8%)
  blocking collectives  37.3 us (7%)
  other arithmetic  34.3 us (6%)
    all_to_all x17, waiting for transfers between devices, swap(): return lax.all_to_all(array, axis, split_axis=0, concat_axis=0, tiled=True)  164 us
    all_to_all x17, starting transfers between devices, swap(): return lax.all_to_all(array, axis, split_axis=0, concat_axis=0, tiled=True)  127 us
    pallas_call x2, Pallas kernels, body(): dense(ritz_kernel, ((modes, 3 * modes), square), modes)  48.2 us
    all_to_all x2, blocking collectives, swap(): return lax.all_to_all(array, axis, split_axis=0, concat_axis=0, tiled=True)  37.3 us
    dot_general x4, matrix products, apply_pair(): jnp.einsum('kcj,kjn->kcn', stacked, blocks, preferred_element_type=jnp.fl...  27.1 us
    concatenate x4, local copies, waits for them, and re-layouts, apply_pair(): stacked = jnp.concatenate(split_three(sources), 1).astype(jnp.bfloat16)  15 us
    pallas_call x1, Pallas kernels, body(): dense(carry_kernel, (pair,) * 4, modes)  14.9 us
    all_to_all x12, other arithmetic, swap(): return lax.all_to_all(array, axis, split_axis=0, concat_axis=0, tiled=True)  12.4 us
  transfers between devices with their start and end apart: 17, of which 13 were waited for; matrix products, arithmetic and copies ran while one was open for 15% of the time, Pallas kernels for 10%

profile of v2, /device:TPU:1, one launch (start us, length us, event | category | flops | bytes accessed | tf_op | source)
XLA Modules:
  0.0 557.2 jit_solution(16147718756425825742)
XLA Ops:
  2.3 10.2 %all-to-all-start.2 = ((f32[8,2,12,512]{3,1,2,0:T(2,128)}), f32[8,2,12,512]{3,1,2,0:T(2,128)S(1)}, u32[]{:S(2)}, u32[]{:S(2)}) async-start(f32[8,2,12,512]{3,1,2,0:T(2,128)} %broadcast_in_dim.656), calls=%async_computation.2 | async-start | bytes 786432 | tf_op jit(solution)/shard_map/all_to_all | solution.py:28
  22.1 14.4 %all-to-all-start = ((f32[64,1,2304]{2,1,0:T(1,128)}), f32[64,1,2304]{2,1,0:T(1,128)}, u32[]{:S(2)}, u32[]{:S(2)}) async-start(f32[64,1,2304]{2,1,0:T(1,128)} %copy.111), calls=%async_computation | async-start | bytes 1179648 | tf_op jit(solution)/shard_map/all_to_all | solution.py:28
  50.4 19.6 %all-to-all-done = f32[64,1,2304]{2,1,0:T(1,128)} async-done(((f32[64,1,2304]{2,1,0:T(1,128)}), f32[64,1,2304]{2,1,0:T(1,128)}, u32[]{:S(2)}, u32[]{:S(2)}) %all-to-all-start) | async-done | bytes 589856 | tf_op jit(solution)/shard_map/all_to_all | solution.py:28
  89.8 7.4 %all-to-all-start.3 = ((f32[64,1,36]{2,1,0:T(1,128)}), f32[64,1,36]{2,1,0:T(1,128)S(1)}, u32[]{:S(2)}, u32[]{:S(2)}) async-start(f32[64,1,36]{2,1,0:T(1,128)} %bitcast.20), calls=%async_computation.3 | async-start | bytes 65536 | tf_op jit(solution)/shard_map/all_to_all | solution.py:28
  97.2 13.3 %all-to-all-done.3 = f32[64,1,36]{2,1,0:T(1,128)S(1)} async-done(((f32[64,1,36]{2,1,0:T(1,128)}), f32[64,1,36]{2,1,0:T(1,128)S(1)}, u32[]{:S(2)}, u32[]{:S(2)}) %all-to-all-start.3) | async-done | bytes 9248 | tf_op jit(solution)/shard_map/all_to_all | solution.py:28
  116.9 12.5 %all-to-all-done.4 = f32[64,1,36]{2,1,0:T(1,128)S(1)} async-done(((f32[64,1,36]{2,1,0:T(1,128)}), f32[64,1,36]{2,1,0:T(1,128)S(1)}, u32[]{:S(2)}, u32[]{:S(2)}) %all-to-all-start.4) | async-done | bytes 9248 | tf_op jit(solution)/shard_map/all_to_all | solution.py:28
  131.4 8.1 %all-to-all-start.5 = ((f32[8,1,2304]{2,1,0:T(1,128)}), f32[8,1,2304]{2,1,0:T(1,128)S(1)}, u32[]{:S(2)}, u32[]{:S(2)}) async-start(f32[8,1,2304]{2,1,0:T(1,128)} %broadcast_in_dim.659), calls=%async_computation.5 | async-start | bytes 147456 | tf_op jit(solution)/shard_map/all_to_all | solution.py:28
  179.3 15.9 %all-to-all-done.10 = f32[64,1,2304]{2,1,0:T(1,128)S(1)} async-done(((f32[64,1,2304]{2,1,0:T(1,128)}), f32[64,1,2304]{2,1,0:T(1,128)S(1)}, u32[]{:S(2)}, u32[]{:S(2)}) %all-to-all-start.10) | async-done | bytes 589856 | tf_op jit(solution)/shard_map/all_to_all | solution.py:28
  195.2 8.5 %all-to-all-start.6 = ((f32[64,1,2304]{2,1,0:T(1,128)}), f32[64,1,2304]{2,1,0:T(1,128)}, u32[]{:S(2)}, u32[]{:S(2)}) async-start(f32[64,1,2304]{2,1,0:T(1,128)} %copy.126), calls=%async_computation.6 | async-start | bytes 1179648 | tf_op jit(solution)/shard_map/all_to_all | solution.py:28
  225.6 9.7 %all-to-all-done.6 = f32[64,1,2304]{2,1,0:T(1,128)} async-done(((f32[64,1,2304]{2,1,0:T(1,128)}), f32[64,1,2304]{2,1,0:T(1,128)}, u32[]{:S(2)}, u32[]{:S(2)}) %all-to-all-start.6) | async-done | bytes 589856 | tf_op jit(solution)/shard_map/all_to_all | solution.py:28
  235.3 9.2 %all-to-all-start.11 = ((f32[64,1,72]{2,1,0:T(1,128)}), f32[64,1,72]{2,1,0:T(1,128)}, u32[]{:S(2)}, u32[]{:S(2)}) async-start(f32[64,1,72]{2,1,0:T(1,128)} %bitcast.28), calls=%async_computation.11 | async-start | bytes 65536 | tf_op jit(solution)/shard_map/all_to_all | solution.py:28
  264.4 14.6 %all-to-all-start.7 = ((f32[64,1,108]{2,1,0:T(1,128)}), f32[64,1,108]{2,1,0:T(1,128)S(1)}, u32[]{:S(2)}, u32[]{:S(2)}) async-start(f32[64,1,108]{2,1,0:T(1,128)} %bitcast.25), calls=%async_computation.7 | async-start | bytes 65536 | tf_op jit(solution)/shard_map/all_to_all | solution.py:28
  279.9 12.5 %all-to-all-done.7 = f32[64,1,108]{2,1,0:T(1,128)S(1)} async-done(((f32[64,1,108]{2,1,0:T(1,128)}), f32[64,1,108]{2,1,0:T(1,128)S(1)}, u32[]{:S(2)}, u32[]{:S(2)}) %all-to-all-start.7) | async-done | bytes 27680 | tf_op jit(solution)/shard_map/all_to_all | solution.py:28
  297.8 13.4 %all-to-all-done.12 = f32[64,1,72]{2,1,0:T(1,128)S(1)} async-done(((f32[64,1,72]{2,1,0:T(1,128)}), f32[64,1,72]{2,1,0:T(1,128)S(1)}, u32[]{:S(2)}, u32[]{:S(2)}) %all-to-all-start.12) | async-done | bytes 18464 | tf_op jit(solution)/shard_map/all_to_all | solution.py:28
  317.3 12.7 %all-to-all-done.8 = f32[64,1,108]{2,1,0:T(1,128)S(1)} async-done(((f32[64,1,108]{2,1,0:T(1,128)}), f32[64,1,108]{2,1,0:T(1,128)S(1)}, u32[]{:S(2)}, u32[]{:S(2)}) %all-to-all-start.8) | async-done | bytes 27680 | tf_op jit(solution)/shard_map/all_to_all | solution.py:28
  330.7 9.1 %all-to-all-start.13 = ((f32[8,1,4608]{2,1,0:T(1,128)}), f32[8,1,4608]{2,1,0:T(1,128)S(1)}, u32[]{:S(2)}, u32[]{:S(2)}) async-start(f32[8,1,4608]{2,1,0:T(1,128)} %broadcast_in_dim.729), calls=%async_computation.13 | async-start | bytes 294912 | tf_op jit(solution)/shard_map/all_to_all | solution.py:28
  363.8 12.1 %shard_map.140 = (f32[192,192]{1,0:T(8,128)}, f32[192,192]{1,0:T(8,128)}, f32[192,192]{1,0:T(8,128)}) custom-call(f32[192,192]{1,0:T(8,128)} %get-tuple-element.104.stiff_ref.gxp_ref, f32[192,192]{1,0:T(8,128)} %get-tuple-element.103.mass_ref.mxp_ref), custom_call_target="tpu_custom_call" | custom-call | tf_op jit(solution)/shard_map/pallas_call | solution.py:320
  378.1 24.2 %shard_map.141 = (f32[96,288]{1,0:T(8,128)}, f32[96,96]{1,0:T(8,128)}) custom-call(f32[96,288]{1,0:T(8,128)} %reshape_squeeze.54.gw_ref, f32[96,288]{1,0:T(8,128)} %reshape_squeeze.55.mw_ref, f32[192,192]{1,0:T(8,128)} %get-tuple-element.103.mass_ref.mxp_ref, f32[192,192]{1,0:T(8,128)} %get-tuple-element.14.j_ref, f32[192,192]{1,0:T(8,128)} %get-tuple-element.15.jm_ref, ...), custom_call_target="tpu_custom_call" | custom-call | tf_op jit(solution)/shard_map/pallas_call | solution.py:329
  416.6 33.0 %all-to-all-done.15 = f32[64,1,2304]{2,1,0:T(1,128)S(1)} async-done(((f32[64,1,2304]{2,1,0:T(1,128)}), f32[64,1,2304]{2,1,0:T(1,128)S(1)}, u32[]{:S(2)}, u32[]{:S(2)}) %all-to-all-start.15) | async-done | bytes 589856 | tf_op jit(solution)/shard_map/all_to_all | solution.py:28
  465.8 20.0 %all_to_all.123 = f32[64,1,108]{2,1,0:T(1,128)S(1)} all-to-all(f32[64,1,108]{2,1,0:T(1,128)S(1)} %bitcast.80), channel_id=1, replica_groups=mesh['rows'=64,'cols'=8] {'rows'}, dimensions={0} | all-to-all | bytes 55296 | tf_op jit(solution)/shard_map/all_to_all | solution.py:28
  485.9 17.4 %all_to_all.124 = f32[64,1,108]{2,1,0:T(1,128)S(1)} all-to-all(f32[64,1,108]{2,1,0:T(1,128)S(1)} %broadcast_in_dim.763), channel_id=1, replica_groups=mesh['rows'=64,'cols'=8] {'rows'}, dimensions={0} | all-to-all | bytes 55296 | tf_op jit(solution)/shard_map/all_to_all | solution.py:28
  505.0 8.4 %all-to-all-start.18 = ((f32[8,1,6912]{2,1,0:T(1,128)}), f32[8,1,6912]{2,1,0:T(1,128)S(1)}, u32[]{:S(2)}, u32[]{:S(2)}) async-start(f32[8,1,6912]{2,1,0:T(1,128)} %broadcast_in_dim.765), calls=%async_computation.18 | async-start | bytes 442368 | tf_op jit(solution)/shard_map/all_to_all | solution.py:28
  513.3 14.9 %shard_map.142 = (f32[192,192]{1,0:T(8,128)}, f32[192,192]{1,0:T(8,128)}, f32[192,192]{1,0:T(8,128)}, f32[192,192]{1,0:T(8,128)}) custom-call(f32[96,288]{1,0:T(8,128)} %get-tuple-element.17.y_ref, f32[192,192]{1,0:T(8,128)} %get-tuple-element.104.stiff_ref.gxp_ref, f32[192,192]{1,0:T(8,128)} %get-tuple-element.103.mass_ref.mxp_ref, ...), custom_call_target="tpu_custom_call" | custom-call | tf_op jit(solution)/shard_map/pallas_call | solution.py:353
  530.3 24.0 %shard_map.143 = (f32[96,288]{1,0:T(8,128)}, f32[96,96]{1,0:T(8,128)}) custom-call(f32[96,288]{1,0:T(8,128)} %reshape_squeeze.62.gw_ref, f32[96,288]{1,0:T(8,128)} %reshape_squeeze.63.mw_ref, f32[192,192]{1,0:T(8,128)} %get-tuple-element.19.mxp_ref, f32[192,192]{1,0:T(8,128)} %get-tuple-element.20.j_ref, f32[192,192]{1,0:T(8,128)} %get-tuple-element.21.jm_ref, ...), custom_call_target="tpu_custom_call" | custom-call | tf_op jit(solution)/shard_map/pallas_call | solution.py:329
  (426 shorter events, 210.0 us)
Async XLA Ops:
  2.3 19.8 %all-to-all-start.2 = ((f32[8,2,12,512]{3,1,2,0:T(2,128)}), f32[8,2,12,512]{3,1,2,0:T(2,128)S(1)}, u32[]{:S(2)}, u32[]{:S(2)}) async-start(f32[8,2,12,512]{3,1,2,0:T(2,128)} %broadcast_in_dim.656), calls=%async_computation.2 | async-start | bytes 786432 | tf_op jit(solution)/shard_map/all_to_all | solution.py:28
  22.1 48.0 %all-to-all-start = ((f32[64,1,2304]{2,1,0:T(1,128)}), f32[64,1,2304]{2,1,0:T(1,128)}, u32[]{:S(2)}, u32[]{:S(2)}) async-start(f32[64,1,2304]{2,1,0:T(1,128)} %copy.111), calls=%async_computation | async-start | bytes 1179648 | tf_op jit(solution)/shard_map/all_to_all | solution.py:28
  39.5 184.7 %copy-start.41 = (s32[72]{0:T(128)}, s32[72]{0:T(128)S(1)}, u32[]{:S(2)}) copy-start(s32[72]{0:T(128)S(1)} %pad_add_fusion.1) | copy-start | bytes 868
  39.6 222.1 %copy-start.36 = (s32[264]{0:T(512)}, s32[264]{0:T(512)S(1)}, u32[]{:S(2)}) copy-start(s32[264]{0:T(512)S(1)} %pad_add_fusion) | copy-start | bytes 3172
  89.8 20.7 %all-to-all-start.3 = ((f32[64,1,36]{2,1,0:T(1,128)}), f32[64,1,36]{2,1,0:T(1,128)S(1)}, u32[]{:S(2)}, u32[]{:S(2)}) async-start(f32[64,1,36]{2,1,0:T(1,128)} %bitcast.20), calls=%async_computation.3 | async-start | bytes 65536 | tf_op jit(solution)/shard_map/all_to_all | solution.py:28
  111.2 18.1 %all-to-all-start.4 = ((f32[64,1,36]{2,1,0:T(1,128)}), f32[64,1,36]{2,1,0:T(1,128)S(1)}, u32[]{:S(2)}, u32[]{:S(2)}) async-start(f32[64,1,36]{2,1,0:T(1,128)} %broadcast_in_dim.657), calls=%async_computation.4 | async-start | bytes 65536 | tf_op jit(solution)/shard_map/all_to_all | solution.py:28
  131.4 13.0 %all-to-all-start.5 = ((f32[8,1,2304]{2,1,0:T(1,128)}), f32[8,1,2304]{2,1,0:T(1,128)S(1)}, u32[]{:S(2)}, u32[]{:S(2)}) async-start(f32[8,1,2304]{2,1,0:T(1,128)} %broadcast_in_dim.659), calls=%async_computation.5 | async-start | bytes 147456 | tf_op jit(solution)/shard_map/all_to_all | solution.py:28
  145.3 12.2 %all-to-all-start.1 = ((f32[8,2,12,512]{3,1,2,0:T(2,128)}), f32[8,2,12,512]{3,1,2,0:T(2,128)S(1)}, u32[]{:S(2)}, u32[]{:S(2)}) async-start(f32[8,2,12,512]{3,1,2,0:T(2,128)} %broadcast_in_dim.655), calls=%async_computation.1 | async-start | bytes 786432 | tf_op jit(solution)/shard_map/all_to_all | solution.py:28
  157.5 37.6 %all-to-all-start.10 = ((f32[64,1,2304]{2,1,0:T(1,128)}), f32[64,1,2304]{2,1,0:T(1,128)S(1)}, u32[]{:S(2)}, u32[]{:S(2)}) async-start(f32[64,1,2304]{2,1,0:T(1,128)} %copy.131), calls=%async_computation.10 | async-start | bytes 1179648 | tf_op jit(solution)/shard_map/all_to_all | solution.py:28
  177.4 27.6 %copy-start.11 = (f32[8,12,512]{2,1,0:T(8,128)S(1)}, f32[8,12,512]{2,1,0:T(8,128)}, u32[]{:S(2)}) copy-start(f32[8,12,512]{2,1,0:T(8,128)} %get-tuple-element.29) | copy-start | bytes 589828
  195.2 40.1 %all-to-all-start.6 = ((f32[64,1,2304]{2,1,0:T(1,128)}), f32[64,1,2304]{2,1,0:T(1,128)}, u32[]{:S(2)}, u32[]{:S(2)}) async-start(f32[64,1,2304]{2,1,0:T(1,128)} %copy.126), calls=%async_computation.6 | async-start | bytes 1179648 | tf_op jit(solution)/shard_map/all_to_all | solution.py:28
  223.0 21.6 %copy-start.23 = (f32[12,8,64]{2,1,0:T(8,128)}, f32[12,8,64]{2,1,0:T(8,128)S(1)}, u32[]{:S(2)}) copy-start(f32[12,8,64]{2,1,0:T(8,128)S(1)} %get-tuple-element.88) | copy-start | bytes 73732
  235.3 29.1 %all-to-all-start.11 = ((f32[64,1,72]{2,1,0:T(1,128)}), f32[64,1,72]{2,1,0:T(1,128)}, u32[]{:S(2)}, u32[]{:S(2)}) async-start(f32[64,1,72]{2,1,0:T(1,128)} %bitcast.28), calls=%async_computation.11 | async-start | bytes 65536 | tf_op jit(solution)/shard_map/all_to_all | solution.py:28
  261.8 88.5 %copy-start.24 = (f32[12,8,64]{2,1,0:T(8,128)S(1)}, f32[12,8,64]{2,1,0:T(8,128)}, u32[]{:S(2)}) copy-start(f32[12,8,64]{2,1,0:T(8,128)} %copy-done.23) | copy-start | bytes 73732
  261.8 88.5 %copy-start.22 = (f32[12,8,64]{2,1,0:T(8,128)S(1)}, f32[12,8,64]{2,1,0:T(8,128)}, u32[]{:S(2)}) copy-start(f32[12,8,64]{2,1,0:T(8,128)} %copy-done.21) | copy-start | bytes 73732
  264.4 28.0 %all-to-all-start.7 = ((f32[64,1,108]{2,1,0:T(1,128)}), f32[64,1,108]{2,1,0:T(1,128)S(1)}, u32[]{:S(2)}, u32[]{:S(2)}) async-start(f32[64,1,108]{2,1,0:T(1,128)} %bitcast.25), calls=%async_computation.7 | async-start | bytes 65536 | tf_op jit(solution)/shard_map/all_to_all | solution.py:28
  293.1 18.1 %all-to-all-start.12 = ((f32[64,1,72]{2,1,0:T(1,128)}), f32[64,1,72]{2,1,0:T(1,128)S(1)}, u32[]{:S(2)}, u32[]{:S(2)}) async-start(f32[64,1,72]{2,1,0:T(1,128)} %broadcast_in_dim.727), calls=%async_computation.12 | async-start | bytes 65536 | tf_op jit(solution)/shard_map/all_to_all | solution.py:28
  311.8 18.1 %all-to-all-start.8 = ((f32[64,1,108]{2,1,0:T(1,128)}), f32[64,1,108]{2,1,0:T(1,128)S(1)}, u32[]{:S(2)}, u32[]{:S(2)}) async-start(f32[64,1,108]{2,1,0:T(1,128)} %broadcast_in_dim.692), calls=%async_computation.8 | async-start | bytes 65536 | tf_op jit(solution)/shard_map/all_to_all | solution.py:28
  330.7 14.5 %all-to-all-start.13 = ((f32[8,1,4608]{2,1,0:T(1,128)}), f32[8,1,4608]{2,1,0:T(1,128)S(1)}, u32[]{:S(2)}, u32[]{:S(2)}) async-start(f32[8,1,4608]{2,1,0:T(1,128)} %broadcast_in_dim.729), calls=%async_computation.13 | async-start | bytes 294912 | tf_op jit(solution)/shard_map/all_to_all | solution.py:28
  346.0 10.3 %all-to-all-start.9 = ((f32[8,1,6912]{2,1,0:T(1,128)}), f32[8,1,6912]{2,1,0:T(1,128)S(1)}, u32[]{:S(2)}, u32[]{:S(2)}) async-start(f32[8,1,6912]{2,1,0:T(1,128)} %broadcast_in_dim.694), calls=%async_computation.9 | async-start | bytes 442368 | tf_op jit(solution)/shard_map/all_to_all | solution.py:28
  357.4 44.9 %all-to-all-start.14 = ((f32[8,4,12,512]{3,1,2,0:T(4,128)}), f32[8,4,12,512]{3,1,2,0:T(4,128)S(1)}, u32[]{:S(2)}, u32[]{:S(2)}) async-start(f32[8,4,12,512]{3,1,2,0:T(4,128)} %broadcast_in_dim.730), calls=%async_computation.14 | async-start | bytes 1572864 | tf_op jit(solution)/shard_map/all_to_all | solution.py:28
  410.3 39.3 %all-to-all-start.15 = ((f32[64,1,2304]{2,1,0:T(1,128)}), f32[64,1,2304]{2,1,0:T(1,128)S(1)}, u32[]{:S(2)}, u32[]{:S(2)}) async-start(f32[64,1,2304]{2,1,0:T(1,128)} %copy.139), calls=%async_computation.15 | async-start | bytes 1179648 | tf_op jit(solution)/shard_map/all_to_all | solution.py:28
  505.0 23.2 %all-to-all-start.18 = ((f32[8,1,6912]{2,1,0:T(1,128)}), f32[8,1,6912]{2,1,0:T(1,128)S(1)}, u32[]{:S(2)}, u32[]{:S(2)}) async-start(f32[8,1,6912]{2,1,0:T(1,128)} %broadcast_in_dim.765), calls=%async_computation.18 | async-start | bytes 442368 | tf_op jit(solution)/shard_map/all_to_all | solution.py:28
  528.2 27.2 %copy-start.1 = (f32[96,1536]{1,0:T(8,128)S(1)}, f32[96,1536]{1,0:T(8,128)}, u32[]{:S(2)}) copy-start(f32[96,1536]{1,0:T(8,128)} %copy-done) | copy-start | bytes 1769476
  (45 other events, 268.5 us)

commit v3 on v2

--- a/solution.py
+++ b/solution.py
@@ -3,8 +3,12 @@
 from jax import lax
 from jax.experimental import pallas as pl
 from jax.experimental.pallas import tpu as pltpu
-from jax.sharding import PartitionSpec as P
-
+from jax.sharding import Mesh, PartitionSpec as P
+
+ROWS = ("z", "y")
+COLS = ("x", "core")
+Y_SIZE = 4
+CORES = 2
 STEPS = 2
 RR_ITERS = 3
 
@@ -41,8 +45,8 @@
     picked = jnp.zeros((slot_ids.shape[0], by_node.shape[1]), jnp.float32)
     for node in range(node_count):
         picked = jnp.where(slot_ids[:, None] == node, by_node[node][None, :], picked)
-    owners = lax.axis_size("rows")
-    received = swap(picked.reshape(owners, -1), "rows")
+    owners = lax.axis_size(ROWS)
+    received = swap(picked.reshape(owners, -1), ROWS)
     return received.reshape(slot_ids.shape[0], col_count, -1)
 
 
@@ -67,14 +71,22 @@
     )
 
 
-def reduce_gram(rows, own_k, own_m, dof_count):
-    own = jnp.concatenate([own_k, own_m], 0)
+def gather_cols(*blocks):
+    count = blocks[0].shape[0]
+    moved = lax.all_gather(jnp.concatenate(blocks, 0), COLS, axis=0)
+    return [
+        moved[:, i * count : (i + 1) * count].reshape(-1, blocks[0].shape[1])
+        for i in range(len(blocks))
+    ]
+
+
+def reduce_gram(rows, own, dof_count):
     part = jnp.einsum("cr,nr->cn", own, rows, precision=exact_dots) / dof_count
-    owners = lax.axis_size("rows")
-    summed = jnp.sum(swap(part.reshape(owners, -1), "rows"), 0)
-    whole = spread(spread(summed, "rows").reshape(-1), "cols")
-    whole = whole.reshape(-1, 2, own_k.shape[0], rows.shape[0])
-    return [whole[:, i].reshape(-1, rows.shape[0]) for i in range(2)]
+    piece = jnp.sum(swap(part.reshape(lax.axis_size("y"), -1), "y"), 0)
+    piece = jnp.sum(spread(piece, "z"), 0)
+    whole = spread(piece, ("y",) + COLS)
+    whole = whole.reshape(lax.axis_size("y"), lax.axis_size(COLS), -1, rows.shape[0])
+    return jnp.swapaxes(whole, 0, 1).reshape(lax.axis_size(COLS), own.shape[0], rows.shape[0])
 
 
 def nn(a, b):
@@ -255,8 +267,8 @@
     iface_live,
 ):
     col_part, row_count = x_start.shape
-    modes = col_part * lax.axis_size("cols")
-    dof_count = row_count * lax.axis_size("rows")
+    modes = col_part * lax.axis_size(COLS)
+    dof_count = row_count * lax.axis_size(ROWS)
     node_count, link_slots = link_to.shape
     node_size = k_diag.shape[1]
     node_ids = jnp.arange(node_count, dtype=jnp.int32)
@@ -293,39 +305,39 @@
     tables = (blocks, src_onehot, dst_onehot, node_count)
 
     precond = 1.0 / jnp.diagonal(k_diag.astype(jnp.float32), axis1=1, axis2=2).reshape(-1)
-    col_start = lax.axis_index("cols") * col_part
-
-    both = spread(jnp.stack([x_start, p_start]), "cols")
-    received_x = exchange(x_start, slot_ids, node_count)
-    received_p = exchange(p_start, slot_ids, node_count)
-    all_x = both[:, 0].reshape(modes, row_count)
-    all_p = both[:, 1].reshape(modes, row_count)
-    own_kx, own_mx = apply_pair(x_start, received_x, tables)
-    stiff_xx, mass_xx = reduce_gram(all_x, own_kx, own_mx, dof_count)
-    moved = spread(jnp.stack([own_kx, own_mx]), "cols")
-    all_kx, all_mx = [moved[:, i].reshape(modes, row_count) for i in range(2)]
-    own_kp, own_mp = apply_pair(p_start, received_p, tables)
-    stiff_p, mass_p = reduce_gram(
-        jnp.concatenate([all_x, all_p], 0), own_kp, own_mp, dof_count
-    )
-
-    def old_block(xx, column):
-        return jnp.concatenate(
-            [jnp.concatenate([xx, column[:, :modes].T], 1), column], 0
-        )
+    col_start = lax.axis_index(COLS) * col_part
+
+    start = jnp.concatenate([x_start, p_start], 0)
+    received = exchange(start, slot_ids, node_count)
+    all_x, all_p = gather_cols(x_start, p_start)
+    own_k, own_m = apply_pair(start, received, tables)
+    products = (own_k[:col_part], own_m[:col_part], own_k[col_part:], own_m[col_part:])
+    gram = reduce_gram(
+        jnp.concatenate([all_x, all_p], 0), jnp.concatenate(products, 0), dof_count
+    )
+    all_kx, all_mx, all_kp, all_mp = gather_cols(*products)
+
+    def block(gram, position):
+        piece = gram[:, position * col_part : (position + 1) * col_part]
+        return piece.reshape(modes, piece.shape[2])
 
     square = (modes, modes)
     pair = (2 * modes, 2 * modes)
-    old_stiff, old_mass = old_block(stiff_xx, stiff_p), old_block(mass_xx, mass_p)
+    old_stiff = jnp.concatenate([block(gram, 0), block(gram, 2)], 0)
+    old_mass = jnp.concatenate([block(gram, 1), block(gram, 3)], 0)
+    (ritz_turned,) = dense(first_ritz_kernel, (square,), modes)(
+        old_stiff[:modes, :modes], old_mass[:modes, :modes]
+    )
     factors = dense(old_kernel, (pair,) * 3, modes)(old_stiff, old_mass)
-    (ritz_turned,) = dense(first_ritz_kernel, (square,), modes)(stiff_xx, mass_xx)
     for step_index in range(STEPS):
         all_w = (all_kx - edot(ritz_turned, all_mx)) * precond[None, :]
         own_w = lax.dynamic_slice_in_dim(all_w, col_start, col_part, 0)
-        received_w = exchange(own_w, slot_ids, node_count)
-        own_kw, own_mw = apply_pair(own_w, received_w, tables)
+        received = exchange(own_w, slot_ids, node_count)
+        received, old_mass, factors = lax.optimization_barrier((received, old_mass, factors))
+        own_kw, own_mw = apply_pair(own_w, received, tables)
         space = jnp.concatenate([all_x, all_p, all_w], 0)
-        stiff_w, mass_w = reduce_gram(space, own_kw, own_mw, dof_count)
+        gram = reduce_gram(space, jnp.concatenate([own_kw, own_mw], 0), dof_count)
+        stiff_w, mass_w = block(gram, 0), block(gram, 1)
         coeffs, ritz_turned = dense(ritz_kernel, ((modes, 3 * modes), square), modes)(
             stiff_w, mass_w, old_mass, *factors
         )
@@ -334,46 +346,34 @@
             p_out = edot(mine[:, modes:], space[modes:])
             x_out = p_out + edot(mine[:, :modes], space[:modes])
             return (x_out, p_out, ritz_turned)
-        moved = spread(jnp.stack([own_kp, own_mp, own_kw, own_mw]), "cols")
-        all_kp, all_mp, all_kw, all_mw = [
-            moved[:, i].reshape(modes, row_count) for i in range(4)
-        ]
-        wide_x = jnp.concatenate([all_x, all_kx, all_mx], 1)
+        all_kw, all_mw = gather_cols(own_kw, own_mw)
+        wide_x = jnp.concatenate([all_kx, all_mx, all_x], 1)
         wide_rest = jnp.concatenate(
             [
-                jnp.concatenate([all_p, all_kp, all_mp], 1),
-                jnp.concatenate([all_w, all_kw, all_mw], 1),
+                jnp.concatenate([all_kp, all_mp, all_p], 1),
+                jnp.concatenate([all_kw, all_mw, all_w], 1),
             ],
             0,
         )
         new_p = edot(coeffs[:, modes:], wide_rest)
         new_x = new_p + edot(coeffs[:, :modes], wide_x)
-        all_x, all_kx, all_mx = [new_x[:, i * row_count : (i + 1) * row_count] for i in range(3)]
-        all_p = new_p[:, :row_count]
+        all_kx, all_mx, all_x = [new_x[:, i * row_count : (i + 1) * row_count] for i in range(3)]
+        all_p = new_p[:, 2 * row_count :]
         old_mass, *factors = dense(carry_kernel, (pair,) * 4, modes)(
             coeffs, old_stiff, old_mass, stiff_w, mass_w
         )
 
 
 def solution(mesh):
-    placed = (
-        P("cols", "rows"),
-        P("cols", "rows"),
-        P("rows", None, None),
-        P("rows", None, None, None),
-        P("rows", None, None),
-        P("rows", None, None, None),
-        P("rows", None),
-        P("rows"),
-        P("rows", None, None, None, None),
-        P("rows", None, None, None, None),
-        P("rows", None, None),
-        P("rows", None, None),
-    )
+    rows, cols = mesh.devices.shape
+    fine = Mesh(
+        mesh.devices.reshape(rows // Y_SIZE, Y_SIZE, cols // CORES, CORES), ROWS + COLS
+    )
+    placed = (P(COLS, ROWS),) * 2 + (P(ROWS),) * 10
     return jax.shard_map(
         body,
-        mesh=mesh,
+        mesh=fine,
         in_specs=placed,
-        out_specs=(P("cols", "rows"), P("cols", "rows"), P()),
+        out_specs=(P(COLS, ROWS), P(COLS, ROWS), P()),
         check_vma=False,
     )

time: 565 us -> 470 us (0.83)
  waiting for transfers between devices: 164 us -> 90.3 us
  starting transfers between devices: 127 us -> 69.6 us
  blocking collectives: 37.3 us -> 89.7 us
  local copies, waits for them, and re-layouts: 67.3 us -> 59.7 us
  other arithmetic: 34.3 us -> 28.4 us
    all_to_all x17 -> x8, waiting for transfers between devices: 164 us -> 90.3 us  [swap(): return lax.all_to_all(array, axis, split_axis=0, concat_axis=0, tiled=True)]
    all_to_all x17 -> x8, starting transfers between devices: 127 us -> 69.6 us  [swap(): return lax.all_to_all(array, axis, split_axis=0, concat_axis=0, tiled=True)]
    all_gather x0 -> x3, blocking collectives: none -> 46.1 us  [gather_cols(): moved = lax.all_gather(jnp.concatenate(blocks, 0), COLS, axis=0)]
    broadcast_in_dim x112 -> x104, local copies, waits for them, and re-layouts: 7.02 us -> 15.9 us  [exchange(): jnp.where(slot_ids[:, None] == node, by_node[node][None, :], picked)]
    all_to_all x2 -> x4, blocking collectives: 37.3 us -> 43.6 us  [swap(): return lax.all_to_all(array, axis, split_axis=0, concat_axis=0, tiled=True)]
    all_to_all x12 -> x6, other arithmetic: 12.4 us -> 7.36 us  [swap(): return lax.all_to_all(array, axis, split_axis=0, concat_axis=0, tiled=True)]
    dot_general x4 -> x3, matrix products: 27.1 us -> 23.9 us  [apply_pair(): jnp.einsum('kcj,kjn->kcn', stacked, blocks, preferred_element_type=jnp.fl...]
    concatenate x4 -> x3, local copies, waits for them, and re-layouts: 15 us -> 13.6 us  [apply_pair(): stacked = jnp.concatenate(split_three(sources), 1).astype(jnp.bfloat16)]
  transfers between devices with their start and end apart: 17 -> 8, of which waited for: 13 -> 6; matrix products, arithmetic and copies ran while one was open for 15% -> 5% of each run, Pallas kernels for 10% -> 6%
where the time goes in v3:
time: 470 us; the launch traced here: 461 us
  waiting for transfers between devices  90.3 us (19%)
  blocking collectives  89.7 us (19%)
  Pallas kernels  81.2 us (17%)
  starting transfers between devices  69.6 us (15%)
  local copies, waits for them, and re-layouts  59.7 us (13%)
  matrix products  39.1 us (8%)
  other arithmetic  28.4 us (6%)
    all_to_all x8, waiting for transfers between devices, swap(): return lax.all_to_all(array, axis, split_axis=0, concat_axis=0, tiled=True)  90.3 us
    all_to_all x8, starting transfers between devices, swap(): return lax.all_to_all(array, axis, split_axis=0, concat_axis=0, tiled=True)  69.6 us
    pallas_call x2, Pallas kernels, body(): dense(ritz_kernel, ((modes, 3 * modes), square), modes)  48.2 us
    all_gather x3, blocking collectives, gather_cols(): moved = lax.all_gather(jnp.concatenate(blocks, 0), COLS, axis=0)  46.1 us
    all_to_all x4, blocking collectives, swap(): return lax.all_to_all(array, axis, split_axis=0, concat_axis=0, tiled=True)  43.6 us
    dot_general x3, matrix products, apply_pair(): jnp.einsum('kcj,kjn->kcn', stacked, blocks, preferred_element_type=jnp.fl...  23.9 us
    broadcast_in_dim x104, local copies, waits for them, and re-layouts, exchange(): jnp.where(slot_ids[:, None] == node, by_node[node][None, :], picked)  15.9 us
    pallas_call x1, Pallas kernels, body(): dense(carry_kernel, (pair,) * 4, modes)  14.9 us
  transfers between devices with their start and end apart: 8, of which 6 were waited for; matrix products, arithmetic and copies ran while one was open for 5% of the time, Pallas kernels for 6%

profile of v3, /device:TPU:1, one launch (start us, length us, event | category | flops | bytes accessed | tf_op | source)
XLA Modules:
  0.0 460.8 jit_solution(11717597607172157361)
XLA Ops:
  17.2 19.3 %all-to-all-start = ((f32[64,1,4608]{2,1,0:T(1,128)}), f32[64,1,4608]{2,1,0:T(1,128)S(1)}, u32[]{:S(2)}, u32[]{:S(2)}) async-start(f32[64,1,4608]{2,1,0:T(1,128)} %copy.241), calls=%async_computation | async-start | bytes 2359296 | tf_op jit(solution)/shard_map/all_to_all | solution.py:32
  39.4 14.3 %all-gather.1 = f32[192,512]{1,0:T(8,128)S(1)} all-gather(f32[24,512]{1,0:T(8,128)S(1)} %pad_maximum_fusion.9), channel_id=3, replica_groups=mesh['z'=16,'y'=4,'x'=4,'core'=2] {'x','core'}, dimensions={0}, use_global_device_ids=true | all-gather | bytes 442368 | tf_op jit(solution)/shard_map/all_gather | solution.py:76
  64.3 29.1 %all-to-all-done = f32[64,1,4608]{2,1,0:T(1,128)S(1)} async-done(((f32[64,1,4608]{2,1,0:T(1,128)}), f32[64,1,4608]{2,1,0:T(1,128)S(1)}, u32[]{:S(2)}, u32[]{:S(2)}) %all-to-all-start) | async-done | bytes 1179680 | tf_op jit(solution)/shard_map/all_to_all | solution.py:32
  107.8 10.2 %fusion.92 = f32[264,72,128]{2,1,0:T(8,128)} fusion(bf16[264,72,64]{1,2,0:T(8,128)(2,1)} %copy.248, bf16[32,64,128]{2,1,0:T(8,128)(2,1)} %get-tuple-element.111, bf16[32,64,128]{2,1,0:T(8,128)(2,1)} %get-tuple-element.110, bf16[8,64,64]{2,1,0:T(8,128)(2,1)} %param.16, bf16[8,64,64]{2,1,0:T(8,128)(2,1)} %param.14, bf16[192,64,128]{2,1,0:T(8,128)(2,1)} %maximum_select_fusion), kind=kOutput, calls=%fused_computation.169 | convolution fusion | flops 333053952 | bytes 16490496 | tf_op jit(solution)/shard_map/kcj,kjn->kcn/dot_general | solution.py:60
  124.9 10.3 %all_to_all.84 = f32[4,1,2304]{2,1,0:T(1,128)S(1)} all-to-all(f32[4,1,2304]{2,1,0:T(1,128)S(1)} %all_to_all.69), channel_id=1, replica_groups=mesh['z'=16,'y'=4,'x'=4,'core'=2] {'y'}, dimensions={0} | all-to-all | bytes 73728 | tf_op jit(solution)/shard_map/all_to_all | solution.py:32
  152.7 10.3 %all-to-all-start.3 = ((f32[32,1,2304]{2,1,0:T(1,128)}), f32[32,1,2304]{2,1,0:T(1,128)S(1)}, u32[]{:S(2)}, u32[]{:S(2)}) async-start(f32[32,1,2304]{2,1,0:T(1,128)} %broadcast_in_dim.554), calls=%async_computation.3 | async-start | bytes 589824 | tf_op jit(solution)/shard_map/all_to_all | solution.py:32
  163.1 15.8 %all-gather = f32[384,512]{1,0:T(8,128)S(1)} all-gather(f32[48,512]{1,0:T(8,128)S(1)} %pad_maximum_fusion.8), channel_id=2, replica_groups=mesh['z'=16,'y'=4,'x'=4,'core'=2] {'x','core'}, dimensions={0}, use_global_device_ids=true | all-gather | bytes 884736 | tf_op jit(solution)/shard_map/all_gather | solution.py:76
  192.6 8.1 %all-to-all-start.4 = ((f32[64,1,2304]{2,1,0:T(1,128)}), f32[64,1,2304]{2,1,0:T(1,128)S(1)}, u32[]{:S(2)}, u32[]{:S(2)}) async-start(f32[64,1,2304]{2,1,0:T(1,128)} %copy.265), calls=%async_computation.4 | async-start | bytes 1179648 | tf_op jit(solution)/shard_map/all_to_all | solution.py:32
  202.2 12.1 %shard_map.140 = (f32[192,192]{1,0:T(8,128)}, f32[192,192]{1,0:T(8,128)}, f32[192,192]{1,0:T(8,128)}) custom-call(f32[192,192]{1,0:T(8,128)} %copy-done.23, f32[192,192]{1,0:T(8,128)} %copy-done.2), custom_call_target="tpu_custom_call" | custom-call | tf_op jit(solution)/shard_map/pallas_call | solution.py:331
  214.8 19.6 %all-to-all-done.4 = f32[64,1,2304]{2,1,0:T(1,128)S(1)} async-done(((f32[64,1,2304]{2,1,0:T(1,128)}), f32[64,1,2304]{2,1,0:T(1,128)S(1)}, u32[]{:S(2)}, u32[]{:S(2)}) %all-to-all-start.4) | async-done | bytes 589856 | tf_op jit(solution)/shard_map/all_to_all | solution.py:32
  241.3 6.9 %fusion.91 = f32[264,36,128]{2,1,0:T(8,128)S(1)} fusion(bf16[264,36,64]{2,1,0:T(8,128)(2,1)} %copy.269, bf16[32,64,128]{2,1,0:T(8,128)(2,1)} %get-tuple-element.111, bf16[32,64,128]{2,1,0:T(8,128)(2,1)S(1)} %copy-done.29, bf16[8,64,64]{2,1,0:T(8,128)(2,1)S(1)} %copy-done.59, bf16[8,64,64]{2,1,0:T(8,128)(2,1)S(1)} %copy-done.34, ...), kind=kOutput, calls=%fused_computation.168 | convolution fusion | flops 177340416 | bytes 10407936 | tf_op jit(solution)/shard_map/kcj,kjn->kcn/dot_general | solution.py:60
  251.0 9.2 %all_to_all.85 = f32[4,1,1728]{2,1,0:T(1,128)S(1)} all-to-all(f32[4,1,1728]{2,1,0:T(1,128)S(1)} %all_to_all.70), channel_id=1, replica_groups=mesh['z'=16,'y'=4,'x'=4,'core'=2] {'y'}, dimensions={0} | all-to-all | bytes 55296 | tf_op jit(solution)/shard_map/all_to_all | solution.py:32
  264.6 15.9 %all-gather.2 = f32[192,512]{1,0:T(8,128)S(1)} all-gather(f32[24,512]{1,0:T(8,128)S(1)} %pad_maximum_fusion.10), channel_id=4, replica_groups=mesh['z'=16,'y'=4,'x'=4,'core'=2] {'x','core'}, dimensions={0}, use_global_device_ids=true | all-gather | bytes 442368 | tf_op jit(solution)/shard_map/all_gather | solution.py:76
  285.2 8.6 %all-to-all-done.7 = f32[32,1,1728]{2,1,0:T(1,128)S(1)} async-done(((f32[32,1,1728]{2,1,0:T(1,128)}), f32[32,1,1728]{2,1,0:T(1,128)S(1)}, u32[]{:S(2)}, u32[]{:S(2)}) %all-to-all-start.7) | async-done | bytes 221216 | tf_op jit(solution)/shard_map/all_to_all | solution.py:32
  296.0 24.2 %shard_map.141 = (f32[96,288]{1,0:T(8,128)}, f32[96,96]{1,0:T(8,128)}) custom-call(f32[96,288]{1,0:T(8,128)} %reshape.1388.gw_ref, f32[96,288]{1,0:T(8,128)} %reshape.1389.mw_ref, f32[192,192]{1,0:T(8,128)} %copy-done.2, f32[192,192]{1,0:T(8,128)} %get-tuple-element.29.j_ref, f32[192,192]{1,0:T(8,128)} %get-tuple-element.30.jm_ref, ...), custom_call_target="tpu_custom_call" | custom-call | tf_op jit(solution)/shard_map/pallas_call | solution.py:341
  326.8 13.5 %all-to-all-start.8 = ((f32[64,1,2304]{2,1,0:T(1,128)}), f32[64,1,2304]{2,1,0:T(1,128)S(1)}, u32[]{:S(2)}, u32[]{:S(2)}) async-start(f32[64,1,2304]{2,1,0:T(1,128)} %copy.276), calls=%async_computation.8 | async-start | bytes 1179648 | tf_op jit(solution)/shard_map/all_to_all | solution.py:32
  340.3 14.9 %shard_map.142 = (f32[192,192]{1,0:T(8,128)}, f32[192,192]{1,0:T(8,128)}, f32[192,192]{1,0:T(8,128)}, f32[192,192]{1,0:T(8,128)}) custom-call(f32[96,288]{1,0:T(8,128)} %get-tuple-element.32.y_ref, f32[192,192]{1,0:T(8,128)} %copy-done.23, f32[192,192]{1,0:T(8,128)} %copy-done.2, f32[96,288]{1,0:T(8,128)} %reshape.1388.gw_ref, f32[96,288]{1,0:T(8,128)} %reshape.1389.mw_ref), custom_call_target="tpu_custom_call" | custom-call | tf_op jit(solution)/shard_map/pallas_call | solution.py:362
  355.7 18.2 %all-to-all-done.8 = f32[64,1,2304]{2,1,0:T(1,128)S(1)} async-done(((f32[64,1,2304]{2,1,0:T(1,128)}), f32[64,1,2304]{2,1,0:T(1,128)S(1)}, u32[]{:S(2)}, u32[]{:S(2)}) %all-to-all-start.8) | async-done | bytes 589856 | tf_op jit(solution)/shard_map/all_to_all | solution.py:32
  381.1 6.7 %fusion.90 = f32[264,36,128]{2,1,0:T(8,128)S(1)} fusion(bf16[264,36,64]{2,1,0:T(8,128)(2,1)} %copy.278, bf16[32,64,128]{2,1,0:T(8,128)(2,1)} %get-tuple-element.111, bf16[32,64,128]{2,1,0:T(8,128)(2,1)S(1)} %copy-done.30, bf16[8,64,64]{2,1,0:T(8,128)(2,1)S(1)} %copy-done.60, bf16[8,64,64]{2,1,0:T(8,128)(2,1)S(1)} %copy-done.35, ...), kind=kOutput, calls=%fused_computation.167 | convolution fusion | flops 177340416 | bytes 10407936 | tf_op jit(solution)/shard_map/kcj,kjn->kcn/dot_general | solution.py:60
  390.2 9.6 %all_to_all.86 = f32[4,1,1728]{2,1,0:T(1,128)S(1)} all-to-all(f32[4,1,1728]{2,1,0:T(1,128)S(1)} %all_to_all.71), channel_id=1, replica_groups=mesh['z'=16,'y'=4,'x'=4,'core'=2] {'y'}, dimensions={0} | all-to-all | bytes 55296 | tf_op jit(solution)/shard_map/all_to_all | solution.py:32
  399.9 14.5 %all_to_all.87 = f32[16,1,1728]{2,1,0:T(1,128)S(1)} all-to-all(f32[16,1,1728]{2,1,0:T(1,128)S(1)} %broadcast_in_dim.635), channel_id=1, replica_groups=mesh['z'=16,'y'=4,'x'=4,'core'=2] {'z'}, dimensions={0} | all-to-all | bytes 221184 | tf_op jit(solution)/shard_map/all_to_all | solution.py:32
  415.3 7.4 %all-to-all-start.11 = ((f32[32,1,1728]{2,1,0:T(1,128)}), f32[32,1,1728]{2,1,0:T(1,128)S(1)}, u32[]{:S(2)}, u32[]{:S(2)}) async-start(f32[32,1,1728]{2,1,0:T(1,128)} %broadcast_in_dim.636), calls=%async_computation.11 | async-start | bytes 458752 | tf_op jit(solution)/shard_map/all_to_all | solution.py:32
  422.7 8.7 %all-to-all-done.11 = f32[32,1,1728]{2,1,0:T(1,128)S(1)} async-done(((f32[32,1,1728]{2,1,0:T(1,128)}), f32[32,1,1728]{2,1,0:T(1,128)S(1)}, u32[]{:S(2)}, u32[]{:S(2)}) %all-to-all-start.11) | async-done | bytes 221216 | tf_op jit(solution)/shard_map/all_to_all | solution.py:32
  433.6 24.0 %shard_map.143 = (f32[96,288]{1,0:T(8,128)}, f32[96,96]{1,0:T(8,128)}) custom-call(f32[96,288]{1,0:T(8,128)} %reshape.1400.gw_ref, f32[96,288]{1,0:T(8,128)} %reshape.1401.mw_ref, f32[192,192]{1,0:T(8,128)} %get-tuple-element.39.mxp_ref, f32[192,192]{1,0:T(8,128)} %get-tuple-element.40.j_ref, f32[192,192]{1,0:T(8,128)} %get-tuple-element.41.jm_ref, ...), custom_call_target="tpu_custom_call" | custom-call | tf_op jit(solution)/shard_map/pallas_call | solution.py:341
  (398 shorter events, 126.5 us)
Async XLA Ops:
  14.9 21.6 %copy-start.56 = (s32[1,64,3]{1,0,2:T(1,128)S(1)}, s32[1,64,3]{1,0,2:T(1,128)}, u32[]{:S(2)}) copy-start(s32[1,64,3]{1,0,2:T(1,128)} %param.22) | copy-start | bytes 2308
  14.9 21.7 %copy-start.57 = (s32[8,4]{0,1:T(4,128)S(1)}, s32[8,4]{0,1:T(4,128)}, u32[]{:S(2)}) copy-start(s32[8,4]{0,1:T(4,128)} %param.18) | copy-start | bytes 388
  14.9 21.9 %copy-start.27 = (bf16[8,4,64,64]{3,2,1,0:T(8,128)(2,1)S(1)}, bf16[8,4,64,64]{3,2,1,0:T(8,128)(2,1)}, u32[]{:S(2)}) copy-start(bf16[8,4,64,64]{3,2,1,0:T(8,128)(2,1)} %param.15) | copy-start | bytes 786436
  14.9 22.2 %copy-start.28 = (bf16[8,4,64,64]{3,2,1,0:T(8,128)(2,1)S(1)}, bf16[8,4,64,64]{3,2,1,0:T(8,128)(2,1)}, u32[]{:S(2)}) copy-start(bf16[8,4,64,64]{3,2,1,0:T(8,128)(2,1)} %param.17) | copy-start | bytes 786436
  17.2 76.2 %all-to-all-start = ((f32[64,1,4608]{2,1,0:T(1,128)}), f32[64,1,4608]{2,1,0:T(1,128)S(1)}, u32[]{:S(2)}, u32[]{:S(2)}) async-start(f32[64,1,4608]{2,1,0:T(1,128)} %copy.241), calls=%async_computation | async-start | bytes 2359296 | tf_op jit(solution)/shard_map/all_to_all | solution.py:32
  135.9 15.8 %all-to-all-start.2 = ((f32[16,1,2304]{2,1,0:T(1,128)}), f32[16,1,2304]{2,1,0:T(1,128)S(1)}, u32[]{:S(2)}, u32[]{:S(2)}) async-start(f32[16,1,2304]{2,1,0:T(1,128)} %broadcast_in_dim.553), calls=%async_computation.2 | async-start | bytes 294912 | tf_op jit(solution)/shard_map/all_to_all | solution.py:32
  141.2 47.3 %copy-start.52 = (f32[512]{0:T(512)}, f32[512]{0:T(512)S(1)}, u32[]{:S(2)}) copy-start(f32[512]{0:T(512)S(1)} %div.29) | copy-start | bytes 6148
  141.8 48.9 %copy-start.7 = (pred[64,1,2304]{2,0,1:T(8,128)(4,1)}, pred[64,1,2304]{2,0,1:T(8,128)(4,1)S(1)}, u32[]{:S(2)}) copy-start(pred[64,1,2304]{2,0,1:T(8,128)(4,1)S(1)} %broadcast_in_dim.499) | copy-start | bytes 442372
  142.3 48.3 %copy-start.9 = (pred[64,1,2304]{2,0,1:T(8,128)(4,1)}, pred[64,1,2304]{2,0,1:T(8,128)(4,1)S(1)}, u32[]{:S(2)}) copy-start(pred[64,1,2304]{2,0,1:T(8,128)(4,1)S(1)} %broadcast_in_dim.560) | copy-start | bytes 442372
  142.9 47.8 %copy-start.11 = (pred[64,1,2304]{2,0,1:T(8,128)(4,1)}, pred[64,1,2304]{2,0,1:T(8,128)(4,1)S(1)}, u32[]{:S(2)}) copy-start(pred[64,1,2304]{2,0,1:T(8,128)(4,1)S(1)} %broadcast_in_dim.566) | copy-start | bytes 442372
  143.4 47.2 %copy-start.13 = (pred[64,1,2304]{2,0,1:T(8,128)(4,1)}, pred[64,1,2304]{2,0,1:T(8,128)(4,1)S(1)}, u32[]{:S(2)}) copy-start(pred[64,1,2304]{2,0,1:T(8,128)(4,1)S(1)} %broadcast_in_dim.572) | copy-start | bytes 442372
  144.0 46.7 %copy-start.15 = (pred[64,1,2304]{2,0,1:T(8,128)(4,1)}, pred[64,1,2304]{2,0,1:T(8,128)(4,1)S(1)}, u32[]{:S(2)}) copy-start(pred[64,1,2304]{2,0,1:T(8,128)(4,1)S(1)} %broadcast_in_dim.578) | copy-start | bytes 442372
  144.5 46.1 %copy-start.17 = (pred[64,1,2304]{2,0,1:T(8,128)(4,1)}, pred[64,1,2304]{2,0,1:T(8,128)(4,1)S(1)}, u32[]{:S(2)}) copy-start(pred[64,1,2304]{2,0,1:T(8,128)(4,1)S(1)} %broadcast_in_dim.584) | copy-start | bytes 442372
  145.1 45.6 %copy-start.19 = (pred[64,1,2304]{2,0,1:T(8,128)(4,1)}, pred[64,1,2304]{2,0,1:T(8,128)(4,1)S(1)}, u32[]{:S(2)}) copy-start(pred[64,1,2304]{2,0,1:T(8,128)(4,1)S(1)} %broadcast_in_dim.590) | copy-start | bytes 442372
  145.6 45.1 %copy-start.21 = (pred[64,1,2304]{2,0,1:T(8,128)(4,1)}, pred[64,1,2304]{2,0,1:T(8,128)(4,1)S(1)}, u32[]{:S(2)}) copy-start(pred[64,1,2304]{2,0,1:T(8,128)(4,1)S(1)} %broadcast_in_dim.596) | copy-start | bytes 442372
  152.7 27.1 %all-to-all-start.3 = ((f32[32,1,2304]{2,1,0:T(1,128)}), f32[32,1,2304]{2,1,0:T(1,128)S(1)}, u32[]{:S(2)}, u32[]{:S(2)}) async-start(f32[32,1,2304]{2,1,0:T(1,128)} %broadcast_in_dim.554), calls=%async_computation.3 | async-start | bytes 589824 | tf_op jit(solution)/shard_map/all_to_all | solution.py:32
  191.2 23.1 %copy-start.55 = (s32[72]{0:T(128)S(1)}, s32[72]{0:T(128)}, u32[]{:S(2)}) copy-start(s32[72]{0:T(128)} %copy-done.54) | copy-start | bytes 868
  192.6 41.8 %all-to-all-start.4 = ((f32[64,1,2304]{2,1,0:T(1,128)}), f32[64,1,2304]{2,1,0:T(1,128)S(1)}, u32[]{:S(2)}, u32[]{:S(2)}) async-start(f32[64,1,2304]{2,1,0:T(1,128)} %copy.265), calls=%async_computation.4 | async-start | bytes 1179648 | tf_op jit(solution)/shard_map/all_to_all | solution.py:32
  261.0 19.5 %all-to-all-start.6 = ((f32[16,1,1728]{2,1,0:T(1,128)}), f32[16,1,1728]{2,1,0:T(1,128)S(1)}, u32[]{:S(2)}, u32[]{:S(2)}) async-start(f32[16,1,1728]{2,1,0:T(1,128)} %broadcast_in_dim.601), calls=%async_computation.6 | async-start | bytes 229376 | tf_op jit(solution)/shard_map/all_to_all | solution.py:32
  281.4 12.4 %all-to-all-start.7 = ((f32[32,1,1728]{2,1,0:T(1,128)}), f32[32,1,1728]{2,1,0:T(1,128)S(1)}, u32[]{:S(2)}, u32[]{:S(2)}) async-start(f32[32,1,1728]{2,1,0:T(1,128)} %broadcast_in_dim.602), calls=%async_computation.7 | async-start | bytes 458752 | tf_op jit(solution)/shard_map/all_to_all | solution.py:32
  323.5 31.7 %copy-start.3 = (f32[96,1536]{1,0:T(8,128)}, f32[96,1536]{1,0:T(8,128)S(1)}, u32[]{:S(2)}) copy-start(f32[96,1536]{1,0:T(8,128)S(1)} %convolution_add_fusion) | copy-start | bytes 1769476
  326.8 47.2 %all-to-all-start.8 = ((f32[64,1,2304]{2,1,0:T(1,128)}), f32[64,1,2304]{2,1,0:T(1,128)S(1)}, u32[]{:S(2)}, u32[]{:S(2)}) async-start(f32[64,1,2304]{2,1,0:T(1,128)} %copy.276), calls=%async_computation.8 | async-start | bytes 1179648 | tf_op jit(solution)/shard_map/all_to_all | solution.py:32
  415.3 16.1 %all-to-all-start.11 = ((f32[32,1,1728]{2,1,0:T(1,128)}), f32[32,1,1728]{2,1,0:T(1,128)S(1)}, u32[]{:S(2)}, u32[]{:S(2)}) async-start(f32[32,1,1728]{2,1,0:T(1,128)} %broadcast_in_dim.636), calls=%async_computation.11 | async-start | bytes 458752 | tf_op jit(solution)/shard_map/all_to_all | solution.py:32
  431.9 26.8 %copy-start.4 = (f32[96,1536]{1,0:T(8,128)S(1)}, f32[96,1536]{1,0:T(8,128)}, u32[]{:S(2)}) copy-start(f32[96,1536]{1,0:T(8,128)} %copy-done.3) | copy-start | bytes 1769476
  (47 other events, 251.8 us)
